TPU v7x, 512 devices: a whole 4x8x8 slice. The times are simulated.
512 devices in a mesh: seq: 64 (over z, x, core), head: 8 (over y).
Axes of the slice: x: 4, y: 8, z: 8, core: 2. Of those that a mesh axis runs over, the one named last changes fastest.
Arguments:
- queries: bfloat16 [65536, 4096], P('seq', 'head'), may hold values from -0.5 to 0.5
- key_rows: bfloat16 [65536, 4096], P('seq', 'head'), may hold values from -6 to 6
- value_rows: bfloat16 [65536, 4096], P('seq', 'head'), may hold values from -6 to 6
- decay_rates: float32 [32], P('head'), as said below
- out_gain: float32 [4096], P('head'), may hold values from 0.5 to 1.5
Outputs:
- attended: bfloat16 [65536, 4096], P('seq', 'head')
Inputs may be any that keep to these rules, and one draw needn't show every extreme that they name: `decay_rates`: positive per-head decay rates.
All inputs are finite; a program needn't handle non-finite values.
Results may differ from a plain program's by a relative error of at most 0.0054.
Values sent between devices are 32-bit elements; how exact they have to be, the bound alone decides.
No kernel may reach another device: no remote copies, remote signals or barrier semaphores. Data moves between devices by JAX's collectives and lax.ppermute only.
A program may use at most 64 MiB of HBM per device.

v0:
```python
import jax
import jax.numpy as jnp
from jax import lax
from jax.sharding import Mesh
from jax.sharding import PartitionSpec as P

H = 32
E = 128
BLOCK = 256
SEQ = ("seq_0", "seq_1", "seq_2")


EPSILON = 1e-06


def filled_with(shard, identity):
    return jax.tree.map(
        lambda a, e: jnp.broadcast_to(jnp.asarray(e, a.dtype), a.shape), shard, identity
    )


def entering_2(shard, axes, combine, identity):
    before = start = filled_with(shard, identity)
    so_far = shard
    for axis in reversed(axes):
        peers, position = (lax.axis_size(axis), lax.axis_index(axis))
        pieces = jax.tree.map(lambda part: lax.all_gather(part, axis), so_far)
        inside, so_far = (start, start)
        for k in range(peers):
            passed = k < position
            so_far = combine(so_far, jax.tree.map(lambda part: part[k], pieces))
            inside = jax.tree.map(lambda new, old: jnp.where(passed, new, old), so_far, inside)
        before = combine(inside, before)
    return before


def from_everyone(shard, axis):
    peers = lax.axis_size(axis)
    return lax.all_to_all(
        jnp.broadcast_to(shard[None], (peers, *shard.shape)), axis, 0, 0, tiled=True
    )


def of_everyone(shard, axis):
    return from_everyone(shard, axis).sum(axis=0)


def combine(earlier, later):
    return (earlier[0] * later[0], later[0][:, None, None] * earlier[1] + later[1])


def body(queries, key_rows, value_rows, decay_rates, out_gain):
    length = queries.shape[0]
    heads = decay_rates.shape[0]
    width = queries.shape[1] // heads
    count = length // BLOCK
    query_blocks = queries.reshape(count, BLOCK, heads, width)
    split_key_blocks = key_rows.reshape(count, BLOCK, heads, width)
    value_blocks = value_rows.reshape(count, BLOCK, heads, width)
    log_decay = -decay_rates
    inner = jnp.arange(BLOCK, dtype=jnp.float32)
    current_block_index = jnp.arange(count, dtype=jnp.float32)
    key_scale = jnp.exp(log_decay[None, :] * (BLOCK - 1 - inner)[:, None])
    decay_scaled_keys = (split_key_blocks * key_scale[None, :, :, None]).astype(jnp.bfloat16)
    stacked_block_states = jnp.einsum(
        "bkhe,bkhf->bhef", decay_scaled_keys, value_blocks, preferred_element_type=jnp.float32
    )
    gap = current_block_index[:, None] - 1.0 - current_block_index[None, :]
    inner_weights = jnp.where(
        gap[:, :, None] >= 0,
        jnp.exp(log_decay[None, None, :] * BLOCK * jnp.maximum(gap, 0.0)[:, :, None]),
        0.0,
    )
    entering = jnp.einsum(
        "iph,phef->ihef", inner_weights, stacked_block_states, precision=lax.Precision.HIGHEST
    )
    tail_weights = jnp.exp(log_decay[None, :] * BLOCK * (count - 1 - current_block_index)[:, None])
    local_state = jnp.einsum(
        "ph,phef->hef", tail_weights, stacked_block_states, precision=lax.Precision.HIGHEST
    )
    block_decay = jnp.exp(log_decay * length)
    unit_decay = jnp.ones_like(block_decay)
    empty_state = jnp.zeros_like(local_state)
    decay_prefix, carried = entering_2(
        (block_decay, local_state), SEQ, combine, (unit_decay, empty_state)
    )
    start_decay = jnp.exp(log_decay[None, :] * BLOCK * current_block_index[:, None])
    carried_half = (start_decay[:, :, None, None] * carried[None] + entering).astype(jnp.bfloat16)
    scores = jnp.einsum(
        "bqhe,bkhe->bhqk", query_blocks, split_key_blocks, preferred_element_type=jnp.float32
    )
    distance = inner[:, None] - inner[None, :]
    masked = jnp.where(
        distance[None] >= 0,
        jnp.exp(log_decay[:, None, None] * jnp.maximum(distance, 0.0)[None]),
        0.0,
    )
    weights_half = (scores * masked[None]).astype(jnp.bfloat16)
    local_out = jnp.einsum(
        "bhqk,bkhe->bqhe", weights_half, value_blocks, preferred_element_type=jnp.float32
    )
    query_scale = jnp.exp(log_decay[None, :] * (inner + 1.0)[:, None])
    carried_out = (
        jnp.einsum(
            "bqhe,bhef->bqhf", query_blocks, carried_half, preferred_element_type=jnp.float32
        )
        * query_scale[None, :, :, None]
    )
    mixed = (local_out + carried_out).reshape(length, heads, width)
    square_sums = of_everyone(jnp.sum(mixed * mixed, axis=(1, 2)), "head")
    inverse = lax.rsqrt(square_sums / (H * E) + EPSILON)
    normed = mixed * inverse[:, None, None] * out_gain.reshape(heads, width)[None]
    return normed.reshape(length, heads * width).astype(jnp.bfloat16)


def solution(mesh):
    torus = Mesh(
        mesh.devices.reshape(8, 4, 2, mesh.shape["head"]), ("seq_0", "seq_1", "seq_2", "head")
    )
    in_specs = (P(SEQ, "head"), P(SEQ, "head"), P(SEQ, "head"), P("head"), P("head"))
    out_specs = P(SEQ, "head")
    return jax.shard_map(body, mesh=torus, in_specs=in_specs, out_specs=out_specs, check_vma=False)
```

profile of v0, /device:TPU:2, one launch (start us, length us, event | category | flops | bytes accessed | tf_op | source)
XLA Modules:
  0.0 143.4 jit_solution(1664370713424150223)
XLA Ops:
  6.5 1.3 dynamic-slice
  8.5 0.8 exponential_dynamic-update-slice_fusion
  9.2 2.4 %all-reduce = f32[8]{0:T(128)S(1)} all-reduce(f32[8]{0:T(128)S(1)} %get-tuple-element.27), channel_id=2, replica_groups=mesh['seq_0'=8,'seq_1'=4,'seq_2'=2,'head'=8] {'seq_2'}, use_global_device_ids=true, to_apply=%add | all-reduce | flops 8 | bytes 64
  11.7 1.3 dynamic-slice.1
  13.6 0.2 fusion.38
  13.8 13.6 %all-reduce.1 = f32[16]{0:T(128)S(1)} all-reduce(f32[16]{0:T(128)S(1)} %get-tuple-element.25), channel_id=4, replica_groups=mesh['seq_0'=8,'seq_1'=4,'seq_2'=2,'head'=8] {'seq_1'}, use_global_device_ids=true, to_apply=%add.1 | all-reduce | flops 16 | bytes 128
  27.4 1.4 reshape.266
  28.8 0.6 copy.36
  29.4 0.3 reshape.267
  29.7 0.1 multiply_exponential_fusion.1
  29.8 0.5 fusion.6
  30.3 2.4 %fusion.8 = f32[4,1,128,128]{3,1,2,0:T(1,128)S(1)} fusion(f32[4,4,1,1]{0,2,3,1:T(1,128)S(1)} %bitcast.76, f32[4,4,128,128]{3,2,1,0:T(8,128)S(1)} %fusion.6), kind=kOutput, calls=%fused_computation.15 | convolution fusion | flops 3145728 | bytes 1310784 | tf_op jit(solution)/shard_map/ph,phef->hef/dot_general | solution.py:78
  32.7 2.2 %all-gather.1 = f32[8,128,128]{2,1,0:T(8,128)S(1)} all-gather(f32[4,128,128]{2,1,0:T(8,128)S(1)} %bitcast.73), channel_id=3, replica_groups=mesh['seq_0'=8,'seq_1'=4,'seq_2'=2,'head'=8] {'seq_2'}, dimensions={0}, use_global_device_ids=true | all-gather | bytes 786432 | tf_op jit(solution)/shard_map/all_gather | solution.py:27
  34.9 0.1 multiply_bitcast_fusion
  35.0 0.7 copy-done.1
  35.7 0.8 fusion.21
  36.6 27.7 %all-gather.7.cloned.1.call-done = f32[4,4,128,128]{3,2,1,0:T(8,128)} async-done(((f32[1,4,128,128]{3,2,1,0:T(8,128)}), f32[4,4,128,128]{3,2,1,0:T(8,128)}) %all-gather.7.cloned.1.call-update) | async-done | bytes 1048592 | tf_op jit(solution)/shard_map/all_gather | solution.py:27
  64.3 2.0 %slice_add_fusion.8 = f32[1,4,128,128]{3,2,1,0:T(8,128)} fusion(f32[4,4,128,128]{3,2,1,0:T(8,128)} %all-gather.7.cloned.1.call-done, f32[4]{0:T(128)S(1)} %get-tuple-element.24, f32[4]{0:T(128)S(1)} %get-tuple-element.23, f32[4]{0:T(128)S(1)} %get-tuple-element.18, f32[4]{0:T(128)S(1)} %get-tuple-element.19), kind=kLoop, calls=%fused_computation.35 | loop fusion | flops 458752 | bytes 1310784 | tf_op jit(solution)/shard_map/add | solution.py:49
  66.4 1.3 reshape.265
  67.7 17.2 %all-gather.3 = f32[8,1,4]{2,1,0:T(1,128)S(1)} all-gather(f32[1,1,4]{2,1,0:T(1,128)S(1)} %get-tuple-element.17), channel_id=1, replica_groups=mesh['seq_0'=8,'seq_1'=4,'seq_2'=2,'head'=8] {'seq_0'}, dimensions={0}, use_global_device_ids=true | all-gather | bytes 144 | tf_op jit(solution)/shard_map/all_gather | solution.py:27
  85.0 0.1 fusion.24
  85.3 1.2 exponential_select_fusion
  86.5 3.9 %fusion.3 = f32[4,4,256,128]{2,3,1,0:T(8,128)} fusion(bf16[4,256,4,128]{1,3,2,0:T(8,128)(2,1)S(1)} %copy.36, f32[4,256,256]{2,1,0:T(8,128)} %exponential_select_fusion, bf16[4,256,4,128]{3,2,1,0:T(4,128)(2,1)S(1)} %reshape.267, bf16[4,256,4,128]{3,2,1,0:T(4,128)(2,1)S(1)} %reshape.265), kind=kOutput, calls=%fused_computation.8 | convolution fusion | flops 538968064 | bytes 6291456 | tf_op jit(solution)/shard_map/bhqk,bkhe->bqhe/dot_general | solution.py:99
  90.4 21.7 %all-gather.9.cloned.1.call-done = f32[8,4,128,128]{3,2,1,0:T(8,128)} async-done(((f32[1,4,128,128]{3,2,1,0:T(8,128)}), f32[8,4,128,128]{3,2,1,0:T(8,128)}) %all-gather.9.cloned.1.call-update) | async-done | bytes 2097168 | tf_op jit(solution)/shard_map/all_gather | solution.py:27
  112.1 2.8 %fusion.20 = f32[4,128,128]{2,1,0:T(8,128)S(1)} fusion(f32[8,4,128,128]{3,2,1,0:T(8,128)} %all-gather.9.cloned.1.call-done, f32[4,4,128,128]{3,2,1,0:T(8,128)} %all-gather.7.cloned.1.call-done, f32[8,128,128]{2,1,0:T(8,128)} %copy-done.1, f32[4]{0:T(128)S(1)} %get-tuple-element.21, f32[4]{0:T(128)S(1)} %get-tuple-element.22, f32[4]{0:T(128)S(1)} %get-tuple-element.18, ...), kind=kLoop, calls=%fused_computation.27 | loop fusion | flops 2818048 | bytes 3932430 | tf_op jit(solution)/shard_map/mul | solution.py:88
  114.9 2.6 %fusion.5 = bf16[4,4,128,128]{3,0,2,1:T(4,128)(2,1)S(1)} fusion(f32[4,4,128,128]{3,2,1,0:T(8,128)S(1)} %copy-done.3, f32[4,128,128]{2,1,0:T(8,128)S(1)} %fusion.20, f32[4,4]{0,1:T(4,128)S(1)} %get-tuple-element.15, f32[4,4]{1,0:T(4,128)S(1)} %fusion.33, f32[4]{0:T(128)S(1)} %get-tuple-element.28, pred[4,4]{1,0:T(4,128)(4,1)S(1)} %fusion.34), kind=kOutput, calls=%fused_computation.11 | convolution fusion | flops 13369472 | bytes 1835168 | tf_op jit(solution)/shard_map/iph,phef->ihef/dot_general | solution.py:74
  117.5 0.6 multiply_reduce_fusion
  118.2 0.6 broadcast_in_dim.42
  118.8 6.8 %all-to-all-start = ((f32[8,1,1024]{2,1,0:T(1,128)}), f32[8,1,1024]{2,1,0:T(1,128)S(1)}, u32[]{:S(2)}, u32[]{:S(2)}) async-start(f32[8,1,1024]{2,1,0:T(1,128)} %broadcast_in_dim.42), calls=%async_computation | async-start | bytes 65536 | tf_op jit(solution)/shard_map/all_to_all | solution.py:39
  125.7 1.8 %copy.41 = f32[4,256,4,128]{3,2,1,0:T(4,128)} copy(f32[4,256,4,128]{1,3,2,0:T(8,128)S(1)} %get-tuple-element.33) | data formatting | bytes 4194304 | tf_op jit(solution)/shard_map/add | solution.py:109
  127.5 6.2 %all-to-all-done = f32[8,1,1024]{2,1,0:T(1,128)S(1)} async-done(((f32[8,1,1024]{2,1,0:T(1,128)}), f32[8,1,1024]{2,1,0:T(1,128)S(1)}, u32[]{:S(2)}, u32[]{:S(2)}) %all-to-all-start) | async-done | bytes 32800 | tf_op jit(solution)/shard_map/all_to_all | solution.py:39
  133.7 2.8 %fusion.1 = bf16[1024,512]{1,0:T(8,128)(2,1)} fusion(f32[128,8,4,128]{3,2,1,0:T(4,128)} %bitcast.72, f32[512]{0:T(512)S(1)} %copy-done.5, f32[1024]{0:T(1024)S(1)} %add_rsqrt_fusion), kind=kLoop, calls=%fused_computation.3 | loop fusion | flops 1572864 | bytes 3151872 | tf_op jit(solution)/shard_map/convert_element_type | solution.py:113
  (28 shorter events, 0.5 us)
Async XLA Ops:
  6.5 57.8 %all-gather.7.cloned.1.call-start = ((), (), s32[]{:S(2)}) async-start(), calls=%async_computation.1 | async-start | bytes 1310720 | tf_op jit(solution)/shard_map/all_gather | solution.py:27
  27.3 2.0 %copy-start.4 = (bf16[1024,512]{1,0:T(8,128)(2,1)S(1)}, bf16[1024,512]{1,0:T(8,128)(2,1)}, u32[]{:S(2)}) copy-start(bf16[1024,512]{1,0:T(8,128)(2,1)} %param.7) | copy-start | bytes 3145732
  30.3 2.4 %copy-start.2 = (f32[4,4,128,128]{3,2,1,0:T(8,128)}, f32[4,4,128,128]{3,2,1,0:T(8,128)S(1)}, u32[]{:S(2)}) copy-start(f32[4,4,128,128]{3,2,1,0:T(8,128)S(1)} %fusion.6) | copy-start | bytes 3145732
  34.9 0.8 copy-start.1
  36.5 75.6 %all-gather.9.cloned.1.call-start = ((), (), s32[]{:S(2)}) async-start(), calls=%async_computation.2 | async-start | bytes 2359296 | tf_op jit(solution)/shard_map/all_gather | solution.py:27
  90.4 24.5 %copy-start.3 = (f32[4,4,128,128]{3,2,1,0:T(8,128)S(1)}, f32[4,4,128,128]{3,2,1,0:T(8,128)}, u32[]{:S(2)}) copy-start(f32[4,4,128,128]{3,2,1,0:T(8,128)} %copy-done.2) | copy-start | bytes 3145732
  112.1 5.4 %copy-start = (f32[4,4,256,128]{2,3,1,0:T(8,128)S(1)}, f32[4,4,256,128]{2,3,1,0:T(8,128)}, u32[]{:S(2)}) copy-start(f32[4,4,256,128]{2,3,1,0:T(8,128)} %fusion.3) | copy-start | bytes 6291460
  118.8 14.9 %all-to-all-start = ((f32[8,1,1024]{2,1,0:T(1,128)}), f32[8,1,1024]{2,1,0:T(1,128)S(1)}, u32[]{:S(2)}, u32[]{:S(2)}) async-start(f32[8,1,1024]{2,1,0:T(1,128)} %broadcast_in_dim.42), calls=%async_computation | async-start | bytes 65536 | tf_op jit(solution)/shard_map/all_to_all | solution.py:39
  125.7 8.1 %copy-start.5 = (f32[512]{0:T(512)S(1)}, f32[512]{0:T(512)}, u32[]{:S(2)}) copy-start(f32[512]{0:T(512)} %param.9) | copy-start | bytes 6148
Sparse Core Ops, SparseCore 0:
  36.6 27.6 all-gather.6
  66.5 45.5 all-gather.8
where the time goes:
time: 144 us; the launch traced here: 143 us
  waiting for transfers between devices  55.6 us (39%)
  blocking collectives  35.4 us (25%)
  between operations  14.9 us (10%)
  other arithmetic  11.1 us (8%)
  matrix products  9.97 us (7%)
  local copies, waits for them, and re-layouts  9.48 us (7%)
  starting transfers between devices  6.88 us (5%)
    all_gather x2, waiting for transfers between devices, entering_2(): pieces = jax.tree.map(lambda part: lax.all_gather(part, axis), so_far)  49.4 us
    all_gather x2, blocking collectives, entering_2(): pieces = jax.tree.map(lambda part: lax.all_gather(part, axis), so_far)  19.4 us
    unnamed x2, blocking collectives  16 us
    all_to_all x1, starting transfers between devices, from_everyone(): lax.all_to_all(jnp.broadcast_to(shard[None], (peers, *shard.shape)), axis...  6.83 us
    all_to_all x1, waiting for transfers between devices, from_everyone(): lax.all_to_all(jnp.broadcast_to(shard[None], (peers, *shard.shape)), axis...  6.18 us
    dot_general x1, matrix products, body(): jnp.einsum('bhqk,bkhe->bqhe', weights_half, value_blocks, preferred_eleme...  3.87 us
    unnamed x17, local copies, waits for them, and re-layouts  3.3 us
  transfers between devices with their start and end apart: 3, of which 3 were waited for; matrix products, arithmetic and copies ran while one was open for 6% of the time, Pallas kernels for 0%

commit v1 on v0

v1 whole, which is shorter than its diff:
```python
import functools

import jax
import jax.numpy as jnp
from jax import lax
from jax.experimental import pallas as pl
from jax.experimental.pallas import tpu as pltpu
from jax.sharding import Mesh
from jax.sharding import PartitionSpec as P

H = 32
E = 128
BLOCK = 256
EPSILON = 1e-06
SEQ = ("z", "x", "c")
CHIPS = ("z", "x")
HEAD = "head"

F32 = jnp.float32
BF16 = jnp.bfloat16
VMEM = pl.BlockSpec(memory_space=pltpu.VMEM)
SMEM = pl.BlockSpec(memory_space=pltpu.SMEM)
HBM = pl.BlockSpec(memory_space=pl.ANY)


def call(kernel, outs, ins, out_specs, scratch=(), limit=24, flops=0, moved=0, name=None):
    return pl.pallas_call(
        kernel,
        out_shape=outs,
        in_specs=ins,
        out_specs=out_specs,
        scratch_shapes=list(scratch),
        compiler_params=pltpu.CompilerParams(vmem_limit_bytes=limit << 20),
        cost_estimate=pl.CostEstimate(flops=flops, bytes_accessed=moved, transcendentals=0),
        name=name,
    )


def power(rate, distance):
    return jnp.exp(-rate * distance)


def head_columns(h):
    return slice(h * E, (h + 1) * E)


def states_kernel(count, heads, rates, keys_hbm, values_hbm, state, before, keys, values, sems):
    def copies(b):
        rows = pl.ds(b * BLOCK, BLOCK)
        return (
            pltpu.make_async_copy(keys_hbm.at[rows], keys.at[rows], sems.at[0, b]),
            pltpu.make_async_copy(values_hbm.at[rows], values.at[rows], sems.at[1, b]),
        )

    for b in range(count):
        for copy in copies(b):
            copy.start()
    inner = lax.broadcasted_iota(jnp.int32, (BLOCK, E), 0).astype(F32)
    for b in range(count):
        rows = pl.ds(b * BLOCK, BLOCK)
        for copy in copies(b):
            copy.wait()
        for h in range(heads):
            rate = rates[h]
            scaled = keys[rows, head_columns(h)].astype(F32) * power(rate, BLOCK - 1.0 - inner)
            block = lax.dot_general(
                scaled.astype(BF16),
                values[rows, head_columns(h)],
                (((0,), (0,)), ((), ())),
                preferred_element_type=F32,
            )
            if b > 0:
                previous = state[h]
                before[b - 1, h] = previous
                block = previous * power(jnp.full((E, E), rate, F32), float(BLOCK)) + block
            state[h] = block


def chip_kernel(length, half, rates, both, total):
    first = lax.axis_index("c") * half
    for i in range(half):
        decay = power(jnp.full((E, E), rates[first + i], F32), float(length))
        total[i] = both[0, first + i] * decay + both[1, first + i]


def scan_kernel(length, half, chips, rates, totals, prefixes):
    piece = lax.axis_index("z") * lax.axis_size("x") + lax.axis_index("x")
    h = lax.axis_index("c") * half + piece // (chips // half)
    decay = power(jnp.full(totals.shape[1:], rates[h], F32), 2.0 * length)
    running = jnp.zeros(totals.shape[1:], F32)
    for i in range(chips):
        prefixes[i] = running
        running = running * decay + totals[i]


def local_kernel(count, heads, rates, queries, keys, values, local):
    row = lax.broadcasted_iota(jnp.int32, (BLOCK, BLOCK), 0)
    column = lax.broadcasted_iota(jnp.int32, (BLOCK, BLOCK), 1)
    distance = (row - column).astype(F32)
    for h in range(heads):
        masked = jnp.where(distance >= 0, power(rates[h], jnp.maximum(distance, 0.0)), 0.0)
        for b in range(count):
            rows = pl.ds(b * BLOCK, BLOCK)
            scores = lax.dot_general(
                queries[rows, head_columns(h)],
                keys[rows, head_columns(h)],
                (((1,), (1,)), ((), ())),
                preferred_element_type=F32,
            )
            weights = (scores * masked).astype(BF16)
            local[rows, head_columns(h)] = jnp.dot(
                weights, values[rows, head_columns(h)], preferred_element_type=F32
            )


def mix_kernel(count, heads, rates, queries, local, prefix, both, before, mixed, squares):
    length = float(count * BLOCK)
    second = lax.axis_index("c") == 1
    inner = lax.broadcasted_iota(jnp.int32, (BLOCK, E), 0).astype(F32)
    entering = []
    for h in range(heads):
        decayed = prefix[h] * power(jnp.full((E, E), rates[h], F32), length) + both[0, h]
        entering.append(jnp.where(second, decayed, prefix[h]))
    for b in range(count):
        rows = pl.ds(b * BLOCK, BLOCK)
        total = jnp.zeros((BLOCK, E), F32)
        for h in range(heads):
            carried = entering[h]
            if b > 0:
                decay = power(jnp.full((E, E), rates[h], F32), float(b * BLOCK))
                carried = carried * decay + before[b - 1, h]
            out = jnp.dot(
                queries[rows, head_columns(h)], carried.astype(BF16), preferred_element_type=F32
            )
            out = local[rows, head_columns(h)] + out * power(rates[h], inner + 1.0)
            mixed[rows, head_columns(h)] = out
            total = total + out * out
        sums = lax.dot_general(
            jnp.ones((8, E), F32),
            total,
            (((1,), (1,)), ((), ())),
            precision=lax.Precision.HIGHEST,
            preferred_element_type=F32,
        )
        for r in range(BLOCK // E):
            row = jnp.broadcast_to(sums[0:1, r * E : (r + 1) * E], (squares.shape[0], E))
            squares[:, b * (BLOCK // E) + r, :] = row


def norm_kernel(count, mixed, squares, gain, out_hbm, out, sems):
    sums = squares[0]
    for i in range(1, squares.shape[0]):
        sums = sums + squares[i]
    inverse = lax.rsqrt(sums / float(H * E) + EPSILON)
    tiles = out.shape[0] // E
    for t in range(tiles):
        rows = pl.ds(t * E, E)
        column = jnp.broadcast_to(inverse[t : t + 1, :], (E, E)).T
        for h in range(out.shape[1] // E):
            part = mixed[rows, head_columns(h)] * column * gain[:, head_columns(h)]
            out[rows, head_columns(h)] = part.astype(BF16)
        if t % 2 == 1:
            pair = pl.ds((t - 1) * E, 2 * E)
            pltpu.make_async_copy(out.at[pair], out_hbm.at[pair], sems.at[t // 2]).start()
    for t in range(1, tiles, 2):
        pair = pl.ds((t - 1) * E, 2 * E)
        pltpu.make_async_copy(out.at[pair], out_hbm.at[pair], sems.at[t // 2]).wait()


def body(queries, key_rows, value_rows, decay_rates, out_gain):
    length, width = queries.shape
    heads = decay_rates.shape[0]
    count = length // BLOCK
    half = heads // 2
    chips = lax.axis_size("z") * lax.axis_size("x")
    parts = lax.axis_size(HEAD)
    shape = jax.ShapeDtypeStruct

    state, before = call(
        functools.partial(states_kernel, count, heads),
        (shape((heads, E, E), F32), shape((count - 1, heads, E, E), F32)),
        [SMEM, HBM, HBM],
        (VMEM, VMEM),
        [
            pltpu.VMEM((length, width), BF16),
            pltpu.VMEM((length, width), BF16),
            pltpu.SemaphoreType.DMA((2, count)),
        ],
        flops=2 * length * E * width,
        moved=4 * length * width,
        name="states",
    )(decay_rates, key_rows, value_rows)
    both = lax.all_gather(state, "c")
    total = call(
        functools.partial(chip_kernel, length, half),
        shape((half, E, E), F32),
        [SMEM, VMEM],
        VMEM,
        name="chip",
    )(decay_rates, both)
    owned = lax.all_to_all(total.reshape(chips, -1, E), CHIPS, 0, 0, tiled=True)
    prefixes = call(
        functools.partial(scan_kernel, length, half, chips),
        shape(owned.shape, F32),
        [SMEM, VMEM],
        VMEM,
        name="scan",
    )(decay_rates, owned)
    mine = lax.all_to_all(prefixes, CHIPS, 0, 0, tiled=True).reshape(half, E, E)
    prefix = lax.all_gather(mine, "c", tiled=True)
    local = call(
        functools.partial(local_kernel, count, heads),
        shape((length, width), F32),
        [SMEM, VMEM, VMEM, VMEM],
        VMEM,
        flops=4 * length * BLOCK * width,
        moved=10 * length * width,
        name="local",
    )(decay_rates, queries, key_rows, value_rows)
    mixed, squares = call(
        functools.partial(mix_kernel, count, heads),
        (shape((length, width), F32), shape((parts, length // E, E), F32)),
        [SMEM, VMEM, VMEM, VMEM, VMEM, VMEM],
        (VMEM, VMEM),
        flops=2 * length * E * width,
        moved=10 * length * width,
        name="mix",
    )(decay_rates, queries, local, prefix, both, before)
    shared = lax.all_to_all(squares, HEAD, 0, 0, tiled=True)
    return call(
        functools.partial(norm_kernel, count),
        shape((length, width), BF16),
        [VMEM, VMEM, VMEM],
        HBM,
        [pltpu.VMEM((length, width), BF16), pltpu.SemaphoreType.DMA((count,))],
        moved=6 * length * width,
        name="norm",
    )(mixed, shared, out_gain.reshape(1, width))


def solution(mesh):
    torus = Mesh(mesh.devices.reshape(8, 4, 2, mesh.shape["head"]), ("z", "x", "c", "head"))
    in_specs = (P(SEQ, "head"), P(SEQ, "head"), P(SEQ, "head"), P("head"), P("head"))
    return jax.shard_map(
        body, mesh=torus, in_specs=in_specs, out_specs=P(SEQ, "head"), check_vma=False
    )
```

time: 144 us -> 68.8 us (0.48)
  the two profiles are of different devices: /device:TPU:2 before, /device:TPU:1 now
where the time goes in v1:
time: 68.8 us; the launch traced here: 68.4 us
  blocking collectives  43.9 us (64%)
  Pallas kernels  8.96 us (13%)
  local copies, waits for them, and re-layouts  8 us (12%)
  starting transfers between devices  3.87 us (6%)
  waiting for transfers between devices  3.61 us (5%)
    all_to_all x1, blocking collectives, body(): owned = lax.all_to_all(total.reshape(chips, -1, E), CHIPS, 0, 0, tiled=True)  16.7 us
    all_to_all x1, blocking collectives, body(): shared = lax.all_to_all(squares, HEAD, 0, 0, tiled=True)  13.6 us
    all_gather x1, blocking collectives, body(): both = lax.all_gather(state, 'c')  8.65 us
    unnamed x18, local copies, waits for them, and re-layouts  8 us
    all_gather x1, blocking collectives, body(): prefix = lax.all_gather(mine, 'c', tiled=True)  4.95 us
    all_to_all x1, starting transfers between devices, body(): mine = lax.all_to_all(prefixes, CHIPS, 0, 0, tiled=True).reshape(half, E, E)  3.87 us
    all_to_all x1, waiting for transfers between devices, body(): mine = lax.all_to_all(prefixes, CHIPS, 0, 0, tiled=True).reshape(half, E, E)  3.61 us
    pallas_call x1, Pallas kernels, body(): call(functools.partial(local_kernel, count, heads), shape((length, width)...  2.04 us
  transfers between devices with their start and end apart: 1, of which 1 were waited for; matrix products, arithmetic and copies ran while one was open for 0% of the time, Pallas kernels for 3%

profile of v1, /device:TPU:1, one launch (start us, length us, event | category | flops | bytes accessed | tf_op | source)
XLA Modules:
  0.0 68.4 jit_solution(9887238040114227039)
XLA Ops:
  0.0 0.0 copy-start.2
  0.0 1.2 %copy-done.2 = bf16[1024,512]{1,0:T(8,128)(2,1)S(1)} copy-done((bf16[1024,512]{1,0:T(8,128)(2,1)S(1)}, bf16[1024,512]{1,0:T(8,128)(2,1)}, u32[]{:S(2)}) %copy-start.2) | copy-done | bytes 1048600
  1.2 0.0 copy-start.4
  1.2 1.2 %copy-done.4 = bf16[1024,512]{1,0:T(8,128)(2,1)S(1)} copy-done((bf16[1024,512]{1,0:T(8,128)(2,1)S(1)}, bf16[1024,512]{1,0:T(8,128)(2,1)}, u32[]{:S(2)}) %copy-start.4) | copy-done | bytes 1048600
  2.5 0.0 copy-start.6
  2.5 0.7 copy-done.6
  3.1 0.0 copy-start.7
  3.1 2.0 %states.1 = (f32[4,128,128]{2,1,0:T(8,128)S(1)}, f32[3,4,128,128]{3,2,1,0:T(8,128)S(1)}) custom-call(f32[4]{0:T(128)S(1)} %copy-done.6, bf16[1024,512]{1,0:T(8,128)(2,1)S(1)} %copy-done.2, bf16[1024,512]{1,0:T(8,128)(2,1)S(1)} %copy-done.4), custom_call_target="tpu_custom_call" | custom-call | flops 134217728 | bytes 2097152 | tf_op jit(solution)/shard_map/states/pallas_call | solution.py:179
  5.1 8.6 %all-gather = f32[8,128,128]{2,1,0:T(8,128)S(1)} all-gather(f32[4,128,128]{2,1,0:T(8,128)S(1)} %get-tuple-element.9), channel_id=2, replica_groups=mesh['z'=8,'x'=4,'c'=2,'head'=8] {'c'}, dimensions={0}, use_global_device_ids=true | all-gather | bytes 786432 | tf_op jit(solution)/shard_map/all_gather | solution.py:193
  13.8 0.6 chip.1
  14.4 16.7 %all_to_all.15.totals = f32[32,8,128]{2,1,0:T(8,128)S(1)} all-to-all(f32[32,8,128]{2,1,0:T(8,128)S(1)} %bitcast.6), channel_id=1, replica_groups=mesh['z'=8,'x'=4,'c'=2,'head'=8] {'z','x'}, dimensions={0} | all-to-all | bytes 262144 | tf_op jit(solution)/shard_map/all_to_all | solution.py:201
  31.1 1.3 %scan.1 = f32[32,8,128]{2,1,0:T(8,128)} custom-call(f32[4]{0:T(128)S(1)} %copy-done.6, f32[32,8,128]{2,1,0:T(8,128)S(1)} %all_to_all.15.totals), custom_call_target="tpu_custom_call" | custom-call | tf_op jit(solution)/shard_map/scan/pallas_call | solution.py:202
  32.3 3.9 %all-to-all-start.1 = ((f32[32,8,128]{2,1,0:T(8,128)}), f32[32,8,128]{2,1,0:T(8,128)S(1)}, u32[]{:S(2)}, u32[]{:S(2)}) async-start(f32[32,8,128]{2,1,0:T(8,128)} %scan.1), calls=%async_computation.1 | async-start | bytes 262144 | tf_op jit(solution)/shard_map/all_to_all | solution.py:209
  36.2 0.0 copy-done.7
  36.2 0.0 copy-start
  36.2 1.2 %copy-done = bf16[1024,512]{1,0:T(8,128)(2,1)S(1)} copy-done((bf16[1024,512]{1,0:T(8,128)(2,1)S(1)}, bf16[1024,512]{1,0:T(8,128)(2,1)}, u32[]{:S(2)}) %copy-start) | copy-done | bytes 1048600
  37.5 0.0 copy-start.3
  37.5 1.2 %copy-done.3 = bf16[1024,512]{1,0:T(8,128)(2,1)S(1)} copy-done((bf16[1024,512]{1,0:T(8,128)(2,1)S(1)}, bf16[1024,512]{1,0:T(8,128)(2,1)}, u32[]{:S(2)}) %copy-start.3) | copy-done | bytes 1048600
  38.7 0.0 copy-start.5
  38.7 1.2 %copy-done.5 = bf16[1024,512]{1,0:T(8,128)(2,1)S(1)} copy-done((bf16[1024,512]{1,0:T(8,128)(2,1)S(1)}, bf16[1024,512]{1,0:T(8,128)(2,1)}, u32[]{:S(2)}) %copy-start.5) | copy-done | bytes 1048600
  39.9 2.0 %local.1 = f32[1024,512]{1,0:T(8,128)S(1)} custom-call(f32[4]{0:T(128)S(1)} %copy-done.7, bf16[1024,512]{1,0:T(8,128)(2,1)S(1)} %copy-done, bf16[1024,512]{1,0:T(8,128)(2,1)S(1)} %copy-done.3, bf16[1024,512]{1,0:T(8,128)(2,1)S(1)} %copy-done.5), custom_call_target="tpu_custom_call" | custom-call | flops 536870912 | bytes 5242880 | tf_op jit(solution)/shard_map/local/pallas_call | solution.py:211
  42.0 3.6 %all-to-all-done.1 = f32[32,8,128]{2,1,0:T(8,128)S(1)} async-done(((f32[32,8,128]{2,1,0:T(8,128)}), f32[32,8,128]{2,1,0:T(8,128)S(1)}, u32[]{:S(2)}, u32[]{:S(2)}) %all-to-all-start.1) | async-done | bytes 131104 | tf_op jit(solution)/shard_map/all_to_all | solution.py:209
  45.6 5.0 %all_gather.11.prefix = f32[4,128,128]{2,1,0:T(8,128)S(1)} all-gather(f32[2,128,128]{2,1,0:T(8,128)S(1)} %bitcast.8), channel_id=1, replica_groups=mesh['z'=8,'x'=4,'c'=2,'head'=8] {'c'}, dimensions={0}, use_global_device_ids=true | all-gather | bytes 393216 | tf_op jit(solution)/shard_map/all_gather | solution.py:210
  50.5 0.0 copy-start.1
  50.5 1.2 %copy-done.1 = bf16[1024,512]{1,0:T(8,128)(2,1)S(1)} copy-done((bf16[1024,512]{1,0:T(8,128)(2,1)S(1)}, bf16[1024,512]{1,0:T(8,128)(2,1)}, u32[]{:S(2)}) %copy-start.1) | copy-done | bytes 1048600
  51.7 0.0 copy-start.8
  51.8 1.9 %mix.1 = (f32[1024,512]{1,0:T(8,128)S(1)}, f32[8,8,128]{2,1,0:T(8,128)S(1)}) custom-call(f32[4]{0:T(128)S(1)} %copy-done.7, bf16[1024,512]{1,0:T(8,128)(2,1)S(1)} %copy-done.1, f32[1024,512]{1,0:T(8,128)S(1)} %local.1, f32[4,128,128]{2,1,0:T(8,128)S(1)} %all_gather.11.prefix, f32[2,4,128,128]{3,2,1,0:T(8,128)S(1)} %bitcast.5, ...), custom_call_target="tpu_custom_call" | custom-call | flops 134217728 | bytes 5242880 | tf_op jit(solution)/shard_map/mix/pallas_call | solution.py:220
  53.6 13.6 %all_to_all.16.squares = f32[8,8,128]{2,1,0:T(8,128)S(1)} all-to-all(f32[8,8,128]{2,1,0:T(8,128)S(1)} %get-tuple-element.12), channel_id=1, replica_groups=mesh['z'=8,'x'=4,'c'=2,'head'=8] {'head'}, dimensions={0} | all-to-all | bytes 65536 | tf_op jit(solution)/shard_map/all_to_all | solution.py:229
  67.2 0.0 copy-done.8
  67.2 1.1 %norm.1 = bf16[1024,512]{1,0:T(8,128)(2,1)} custom-call(f32[1024,512]{1,0:T(8,128)S(1)} %get-tuple-element.11.mixed, f32[8,8,128]{2,1,0:T(8,128)S(1)} %all_to_all.16.squares, f32[1,512]{1,0:T(1,128)S(1)} %bitcast.7), custom_call_target="tpu_custom_call" | custom-call | bytes 3145728 | tf_op jit(solution)/shard_map/norm/pallas_call | solution.py:230
Async XLA Ops:
  0.0 1.2 %copy-start.2 = (bf16[1024,512]{1,0:T(8,128)(2,1)S(1)}, bf16[1024,512]{1,0:T(8,128)(2,1)}, u32[]{:S(2)}) copy-start(bf16[1024,512]{1,0:T(8,128)(2,1)} %keys_hbm.1) | copy-start | bytes 3145732
  1.2 1.2 %copy-start.4 = (bf16[1024,512]{1,0:T(8,128)(2,1)S(1)}, bf16[1024,512]{1,0:T(8,128)(2,1)}, u32[]{:S(2)}) copy-start(bf16[1024,512]{1,0:T(8,128)(2,1)} %values_hbm.1) | copy-start | bytes 3145732
  2.5 0.7 copy-start.6
  3.1 33.1 %copy-start.7 = (f32[4]{0:T(128)S(1)}, f32[4]{0:T(128)}, u32[]{:S(2)}) copy-start(f32[4]{0:T(128)} %rates.9) | copy-start | bytes 52
  32.3 13.2 %all-to-all-start.1 = ((f32[32,8,128]{2,1,0:T(8,128)}), f32[32,8,128]{2,1,0:T(8,128)S(1)}, u32[]{:S(2)}, u32[]{:S(2)}) async-start(f32[32,8,128]{2,1,0:T(8,128)} %scan.1), calls=%async_computation.1 | async-start | bytes 262144 | tf_op jit(solution)/shard_map/all_to_all | solution.py:209
  36.2 1.2 %copy-start = (bf16[1024,512]{1,0:T(8,128)(2,1)S(1)}, bf16[1024,512]{1,0:T(8,128)(2,1)}, u32[]{:S(2)}) copy-start(bf16[1024,512]{1,0:T(8,128)(2,1)} %queries.3) | copy-start | bytes 3145732
  37.5 1.2 %copy-start.3 = (bf16[1024,512]{1,0:T(8,128)(2,1)S(1)}, bf16[1024,512]{1,0:T(8,128)(2,1)}, u32[]{:S(2)}) copy-start(bf16[1024,512]{1,0:T(8,128)(2,1)} %keys_hbm.1) | copy-start | bytes 3145732
  38.7 1.2 %copy-start.5 = (bf16[1024,512]{1,0:T(8,128)(2,1)S(1)}, bf16[1024,512]{1,0:T(8,128)(2,1)}, u32[]{:S(2)}) copy-start(bf16[1024,512]{1,0:T(8,128)(2,1)} %values_hbm.1) | copy-start | bytes 3145732
  50.5 1.2 %copy-start.1 = (bf16[1024,512]{1,0:T(8,128)(2,1)S(1)}, bf16[1024,512]{1,0:T(8,128)(2,1)}, u32[]{:S(2)}) copy-start(bf16[1024,512]{1,0:T(8,128)(2,1)} %queries.3) | copy-start | bytes 3145732
  51.7 15.5 %copy-start.8 = (f32[512]{0:T(512)S(1)}, f32[512]{0:T(512)}, u32[]{:S(2)}) copy-start(f32[512]{0:T(512)} %param.9) | copy-start | bytes 6148

commit v2 on v1

v2 whole, which is shorter than its diff:
```python
import functools

import jax
import jax.numpy as jnp
from jax import lax
from jax.experimental import pallas as pl
from jax.experimental.pallas import tpu as pltpu
from jax.sharding import Mesh
from jax.sharding import PartitionSpec as P

H = 32
E = 128
BLOCK = 256
EPSILON = 1e-06
SEQ = ("z", "x", "c")
CHIPS = ("z", "x")
HEAD = "head"

F32 = jnp.float32
BF16 = jnp.bfloat16
VMEM_BYTES = 67043328
STATES_ROOM = 11 << 20
LOCAL_ROOM = 30 << 20
VMEM = pl.BlockSpec(memory_space=pltpu.VMEM)
HBM = pl.BlockSpec(memory_space=pltpu.HBM)


def call(kernel, outs, ins, out_specs, scratch=(), room=40 << 20, flops=0, moved=0, name=None):
    return pl.pallas_call(
        kernel,
        out_shape=outs,
        in_specs=ins,
        out_specs=out_specs,
        scratch_shapes=list(scratch),
        compiler_params=pltpu.CompilerParams(vmem_limit_bytes=VMEM_BYTES - room),
        cost_estimate=pl.CostEstimate(flops=flops, bytes_accessed=moved, transcendentals=0),
        name=name,
    )


def power(rate, distance):
    return jnp.exp(-rate * distance)


def head_columns(h):
    return slice(h * E, (h + 1) * E)


def states_kernel(
    count, heads, rates_hbm, keys_hbm, values_hbm, state, wide, keys, values, scale, rates, sems, rate_sem
):
    def copies(b):
        rows = pl.ds(b * BLOCK, BLOCK)
        return (
            pltpu.make_async_copy(keys_hbm.at[rows], keys.at[rows], sems.at[0, b]),
            pltpu.make_async_copy(values_hbm.at[rows], values.at[rows], sems.at[1, b]),
        )

    rate_copy = pltpu.make_async_copy(rates_hbm, rates, rate_sem)
    rate_copy.start()
    for b in range(count):
        for copy in copies(b):
            copy.start()
    inner = lax.broadcasted_iota(jnp.int32, (BLOCK, E), 0).astype(F32)
    rate_copy.wait()
    for h in range(heads):
        wide[h] = jnp.full((8, E), rates[h], F32)
        scale[h] = power(rates[h], BLOCK - 1.0 - inner)
    for b in range(count):
        rows = pl.ds(b * BLOCK, BLOCK)
        for copy in copies(b):
            copy.wait()
        for h in range(heads):
            scaled = keys[rows, head_columns(h)].astype(F32) * scale[h]
            block = lax.dot_general(
                scaled.astype(BF16),
                values[rows, head_columns(h)],
                (((0,), (0,)), ((), ())),
                preferred_element_type=F32,
            )
            if b > 0:
                block = state[h] * power(wide[h, 0:1], float(BLOCK)) + block
            state[h] = block


def chip_kernel(length, half, wide, both, total):
    first = lax.axis_index("c") * half
    for i in range(half):
        decay = power(wide[first + i, 0:1], float(length))
        total[i] = both[0, first + i] * decay + both[1, first + i]


def scan_kernel(length, half, chips, wide, totals, prefixes):
    piece = lax.axis_index("z") * lax.axis_size("x") + lax.axis_index("x")
    h = lax.axis_index("c") * half + piece // (chips // half)
    decay = power(wide[h], 2.0 * length)
    running = jnp.zeros(totals.shape[1:], F32)
    for i in range(chips):
        prefixes[i] = running
        running = running * decay + totals[i]


def two_halves(matrix):
    high = matrix.astype(BF16)
    low = (matrix - high.astype(F32)).astype(BF16)
    return jnp.concatenate([high, low], axis=0)


def local_kernel(
    count, heads, wide, both, queries_hbm, keys_hbm, values_hbm, local, queries, keys, values, sems
):
    def copies(b):
        rows = pl.ds(b * BLOCK, BLOCK)
        pairs = ((queries_hbm, queries), (keys_hbm, keys), (values_hbm, values))
        return [
            pltpu.make_async_copy(source.at[rows], target.at[rows], sems.at[i, b])
            for i, (source, target) in enumerate(pairs)
        ]

    for b in range(count):
        for copy in copies(b):
            copy.start()
    second = lax.axis_index("c") == 1
    inner = lax.broadcasted_iota(jnp.int32, (BLOCK, E), 0).astype(F32)
    row = lax.broadcasted_iota(jnp.int32, (BLOCK, BLOCK), 0)
    column = lax.broadcasted_iota(jnp.int32, (BLOCK, BLOCK), 1)
    distance = (row - column).astype(F32)
    for b in range(count):
        for copy in copies(b):
            copy.wait()
    for h in range(heads):
        rate = jnp.concatenate([wide[h, 0:1]] * (BLOCK // E), axis=1)
        masked = jnp.where(distance >= 0, power(rate, jnp.maximum(distance, 0.0)), 0.0)
        scale = power(wide[h, 0:1], inner + 1.0)
        key_scale = power(wide[h, 0:1], BLOCK - 1.0 - inner)
        held = jnp.where(second, both[0, h], 0.0)
        for b in range(count):
            rows = pl.ds(b * BLOCK, BLOCK)
            query = queries[rows, head_columns(h)]
            scores = lax.dot_general(
                query, keys[rows, head_columns(h)], (((1,), (1,)), ((), ())), preferred_element_type=F32
            )
            weights = (scores * masked).astype(BF16)
            out = jnp.dot(weights, values[rows, head_columns(h)], preferred_element_type=F32)
            doubled = jnp.concatenate([query, query], axis=1)
            carried = jnp.dot(doubled, two_halves(held), preferred_element_type=F32)
            local[rows, head_columns(h)] = out + carried * scale
            if b < count - 1:
                scaled = keys[rows, head_columns(h)].astype(F32) * key_scale
                block = lax.dot_general(
                    scaled.astype(BF16),
                    values[rows, head_columns(h)],
                    (((0,), (0,)), ((), ())),
                    preferred_element_type=F32,
                )
                held = held * power(wide[h, 0:1], float(BLOCK)) + block


def mix_kernel(count, heads, wide, queries, local, prefix, mixed, squares, scale):
    length = float(count * BLOCK)
    second = lax.axis_index("c") == 1
    inner = lax.broadcasted_iota(jnp.int32, (BLOCK, E), 0).astype(F32)
    entering = []
    for h in range(heads):
        scale[h] = power(wide[h, 0:1], inner + 1.0)
        entering.append(two_halves(prefix[h] * jnp.where(second, power(wide[h, 0:1], length), 1.0)))
    for b in range(count):
        rows = pl.ds(b * BLOCK, BLOCK)
        total = jnp.zeros((BLOCK, E), F32)
        for h in range(heads):
            query = queries[rows, head_columns(h)]
            doubled = jnp.concatenate([query, query], axis=1)
            out = jnp.dot(doubled, entering[h], preferred_element_type=F32)
            factor = scale[h] * power(wide[h, 0:1], float(b * BLOCK)) if b > 0 else scale[h]
            out = local[rows, head_columns(h)] + out * factor
            mixed[rows, head_columns(h)] = out
            total = total + out * out
        sums = lax.dot_general(
            jnp.ones((8, E), F32),
            total,
            (((1,), (1,)), ((), ())),
            precision=lax.Precision.HIGHEST,
            preferred_element_type=F32,
        )
        for r in range(BLOCK // E):
            row = jnp.broadcast_to(sums[0:1, r * E : (r + 1) * E], (squares.shape[0], E))
            squares[:, b * (BLOCK // E) + r, :] = row


def norm_kernel(count, mixed, squares, gain, out_hbm, out, sems):
    sums = squares[0]
    for i in range(1, squares.shape[0]):
        sums = sums + squares[i]
    inverse = lax.rsqrt(sums / float(H * E) + EPSILON)
    tiles = out.shape[0] // E
    for t in range(tiles):
        rows = pl.ds(t * E, E)
        column = jnp.broadcast_to(inverse[t : t + 1, :], (E, E)).T
        for h in range(out.shape[1] // E):
            part = mixed[rows, head_columns(h)] * column * gain[:, head_columns(h)]
            out[rows, head_columns(h)] = part.astype(BF16)
        if t % 2 == 1:
            pair = pl.ds((t - 1) * E, 2 * E)
            pltpu.make_async_copy(out.at[pair], out_hbm.at[pair], sems.at[t // 2]).start()
    for t in range(1, tiles, 2):
        pair = pl.ds((t - 1) * E, 2 * E)
        pltpu.make_async_copy(out.at[pair], out_hbm.at[pair], sems.at[t // 2]).wait()


def body(queries, key_rows, value_rows, decay_rates, out_gain):
    length, width = queries.shape
    heads = decay_rates.shape[0]
    count = length // BLOCK
    half = heads // 2
    chips = lax.axis_size("z") * lax.axis_size("x")
    parts = lax.axis_size(HEAD)
    shape = jax.ShapeDtypeStruct

    state, wide = call(
        functools.partial(states_kernel, count, heads),
        (
            shape((heads, E, E), F32),
            shape((heads, 8, E), F32),
        ),
        [HBM, HBM, HBM],
        (VMEM, VMEM),
        [
            pltpu.VMEM((length, width), BF16),
            pltpu.VMEM((length, width), BF16),
            pltpu.VMEM((heads, BLOCK, E), F32),
            pltpu.SMEM((heads,), F32),
            pltpu.SemaphoreType.DMA((2, count)),
            pltpu.SemaphoreType.DMA,
        ],
        room=STATES_ROOM,
        flops=2 * length * E * width,
        moved=4 * length * width,
        name="states",
    )(decay_rates, key_rows, value_rows)
    both = lax.all_gather(state, "c")
    total = call(
        functools.partial(chip_kernel, length, half),
        shape((half, E, E), F32),
        [VMEM, VMEM],
        VMEM,
        name="chip",
    )(wide, both)
    owned = lax.all_to_all(total.reshape(chips, -1, E), CHIPS, 0, 0, tiled=True)
    prefixes = call(
        functools.partial(scan_kernel, length, half, chips),
        shape(owned.shape, F32),
        [VMEM, VMEM],
        VMEM,
        name="scan",
    )(wide, owned)
    mine = lax.all_to_all(prefixes, CHIPS, 0, 0, tiled=True).reshape(half, E, E)
    prefix = lax.all_gather(mine, "c", tiled=True)
    local, staged = call(
        functools.partial(local_kernel, count, heads),
        (shape((length, width), F32), shape((length, width), BF16)),
        [VMEM, VMEM, HBM, HBM, HBM],
        (VMEM, VMEM),
        [
            pltpu.VMEM((length, width), BF16),
            pltpu.VMEM((length, width), BF16),
            pltpu.SemaphoreType.DMA((3, count)),
        ],
        room=LOCAL_ROOM,
        flops=1 << 40,
        moved=0,
        name="local",
    )(wide, both, queries, key_rows, value_rows)
    mixed, squares = call(
        functools.partial(mix_kernel, count, heads),
        (shape((length, width), F32), shape((parts, length // E, E), F32)),
        [VMEM] * 4,
        (VMEM, VMEM),
        [pltpu.VMEM((heads, BLOCK, E), F32)],
        flops=4 * length * E * width,
        moved=10 * length * width,
        name="mix",
    )(wide, staged, local, prefix)
    shared = lax.all_to_all(squares, HEAD, 0, 0, tiled=True)
    return call(
        functools.partial(norm_kernel, count),
        shape((length, width), BF16),
        [VMEM, VMEM, VMEM],
        HBM,
        [pltpu.VMEM((length, width), BF16), pltpu.SemaphoreType.DMA((count,))],
        moved=6 * length * width,
        name="norm",
    )(mixed, shared, out_gain.reshape(1, width))


def solution(mesh):
    torus = Mesh(mesh.devices.reshape(8, 4, 2, mesh.shape["head"]), ("z", "x", "c", "head"))
    in_specs = (P(SEQ, "head"), P(SEQ, "head"), P(SEQ, "head"), P("head"), P("head"))
    return jax.shard_map(
        body, mesh=torus, in_specs=in_specs, out_specs=P(SEQ, "head"), check_vma=False
    )
```

time: 68.8 us -> 66.2 us (0.962)
  waiting for transfers between devices: 3.61 us -> 0.99 us
  local copies, waits for them, and re-layouts: 8 us -> 6.52 us
  starting transfers between devices: 3.87 us -> 4.56 us
    all_to_all x1, waiting for transfers between devices: 3.61 us -> 0.99 us  [body(): mine = lax.all_to_all(prefixes, CHIPS, 0, 0, tiled=True).reshape(half, E, E)]
    pallas_call x1, Pallas kernels: 2.04 us -> 3.73 us  [body(): call(functools.partial(local_kernel, count, heads), (shape((length, width...]
    unnamed x18 -> x14, local copies, waits for them, and re-layouts: 8 us -> 6.52 us
    all_to_all x1, starting transfers between devices: 3.87 us -> 4.56 us  [body(): mine = lax.all_to_all(prefixes, CHIPS, 0, 0, tiled=True).reshape(half, E, E)]
  transfers between devices with their start and end apart: 1 -> 1, of which waited for: 1 -> 1; matrix products, arithmetic and copies ran while one was open for 0% -> 0% of each run, Pallas kernels for 3% -> 6%
where the time goes in v2:
time: 66.2 us; the launch traced here: 65.8 us
  blocking collectives  44 us (66%)
  Pallas kernels  9.61 us (15%)
  local copies, waits for them, and re-layouts  6.52 us (10%)
  starting transfers between devices  4.56 us (7%)
  waiting for transfers between devices  0.99 us (1%)
    all_to_all x1, blocking collectives, body(): owned = lax.all_to_all(total.reshape(chips, -1, E), CHIPS, 0, 0, tiled=True)  16.7 us
    all_to_all x1, blocking collectives, body(): shared = lax.all_to_all(squares, HEAD, 0, 0, tiled=True)  13.6 us
    all_gather x1, blocking collectives, body(): both = lax.all_gather(state, 'c')  8.65 us
    unnamed x14, local copies, waits for them, and re-layouts  6.52 us
    all_gather x1, blocking collectives, body(): prefix = lax.all_gather(mine, 'c', tiled=True)  5.11 us
    all_to_all x1, starting transfers between devices, body(): mine = lax.all_to_all(prefixes, CHIPS, 0, 0, tiled=True).reshape(half, E, E)  4.56 us
    pallas_call x1, Pallas kernels, body(): call(functools.partial(local_kernel, count, heads), (shape((length, width...  3.73 us
    pallas_call x1, Pallas kernels, body(): call(functools.partial(states_kernel, count, heads), (shape((heads, E, E)...  2.23 us
  transfers between devices with their start and end apart: 1, of which 1 were waited for; matrix products, arithmetic and copies ran while one was open for 0% of the time, Pallas kernels for 6%

profile of v2, /device:TPU:1, one launch (start us, length us, event | category | flops | bytes accessed | tf_op | source)
XLA Modules:
  0.0 65.8 jit_solution(891215836704359599)
XLA Ops:
  0.0 0.0 copy-start.5
  0.0 0.7 copy-done.5
  0.7 2.2 %states.1 = (f32[4,128,128]{2,1,0:T(8,128)S(1)}, f32[4,8,128]{2,1,0:T(8,128)S(1)}) custom-call(f32[4]{0:T(128)S(1)} %copy-done.5, bf16[1024,512]{1,0:T(8,128)(2,1)} %keys_hbm.3, bf16[1024,512]{1,0:T(8,128)(2,1)} %values_hbm.3), custom_call_target="tpu_custom_call" | custom-call | flops 134217728 | bytes 2097152 | tf_op jit(solution)/shard_map/states/pallas_call | solution.py:219
  2.9 8.6 %all-gather = f32[8,128,128]{2,1,0:T(8,128)S(1)} all-gather(f32[4,128,128]{2,1,0:T(8,128)S(1)} %get-tuple-element.12), channel_id=2, replica_groups=mesh['z'=8,'x'=4,'c'=2,'head'=8] {'c'}, dimensions={0}, use_global_device_ids=true | all-gather | bytes 786432 | tf_op jit(solution)/shard_map/all_gather | solution.py:240
  11.6 16.7 %all_to_all.15.totals = f32[32,8,128]{2,1,0:T(8,128)S(1)} all-to-all(f32[32,8,128]{2,1,0:T(8,128)S(1)} %bitcast.6), channel_id=1, replica_groups=mesh['z'=8,'x'=4,'c'=2,'head'=8] {'z','x'}, dimensions={0} | all-to-all | bytes 262144 | tf_op jit(solution)/shard_map/all_to_all | solution.py:248
  28.3 0.7 %scan.1 = f32[32,8,128]{2,1,0:T(8,128)} custom-call(f32[4,8,128]{2,1,0:T(8,128)S(1)} %get-tuple-element.11.wide, f32[32,8,128]{2,1,0:T(8,128)S(1)} %all_to_all.15.totals), custom_call_target="tpu_custom_call" | custom-call | tf_op jit(solution)/shard_map/scan/pallas_call | solution.py:249
  29.0 4.6 %all-to-all-start.1 = ((f32[32,8,128]{2,1,0:T(8,128)}), f32[32,8,128]{2,1,0:T(8,128)}, u32[]{:S(2)}, u32[]{:S(2)}) async-start(f32[32,8,128]{2,1,0:T(8,128)} %scan.1), calls=%async_computation.1 | async-start | bytes 262144 | tf_op jit(solution)/shard_map/all_to_all | solution.py:256
  33.6 0.0 copy-start
  33.6 1.2 %copy-done = bf16[1024,512]{1,0:T(8,128)(2,1)S(1)} copy-done((bf16[1024,512]{1,0:T(8,128)(2,1)S(1)}, bf16[1024,512]{1,0:T(8,128)(2,1)}, u32[]{:S(2)}) %copy-start) | copy-done | bytes 1048600
  34.8 0.0 copy-start.1
  34.8 1.2 %copy-done.1 = bf16[1024,512]{1,0:T(8,128)(2,1)S(1)} copy-done((bf16[1024,512]{1,0:T(8,128)(2,1)S(1)}, bf16[1024,512]{1,0:T(8,128)(2,1)}, u32[]{:S(2)}) %copy-start.1) | copy-done | bytes 1048600
  36.0 0.0 copy-start.6
  36.0 1.2 %copy-done.6 = bf16[1024,512]{1,0:T(8,128)(2,1)S(1)} copy-done((bf16[1024,512]{1,0:T(8,128)(2,1)S(1)}, bf16[1024,512]{1,0:T(8,128)(2,1)}, u32[]{:S(2)}) %copy-start.6) | copy-done | bytes 1048600
  37.2 3.7 %local.1 = (f32[1024,512]{1,0:T(8,128)S(1)}, bf16[1024,512]{1,0:T(8,128)(2,1)S(1)}) custom-call(f32[4,8,128]{2,1,0:T(8,128)S(1)} %get-tuple-element.11.wide, f32[2,4,128,128]{3,2,1,0:T(8,128)S(1)} %bitcast.5, bf16[1024,512]{1,0:T(8,128)(2,1)S(1)} %copy-done.6, bf16[1024,512]{1,0:T(8,128)(2,1)S(1)} %copy-done, bf16[1024,512]{1,0:T(8,128)(2,1)S(1)} %copy-done.1), custom_call_target="tpu_custom_call" | custom-call | flops 1099511627776 | tf_op jit(solution)/shard_map/local/pallas_call | solution.py:258
  41.0 0.0 copy-start.2
  41.0 1.0 %copy-done.2 = bf16[1024,512]{1,0:T(8,128)(2,1)} copy-done((bf16[1024,512]{1,0:T(8,128)(2,1)}, bf16[1024,512]{1,0:T(8,128)(2,1)S(1)}, u32[]{:S(2)}) %copy-start.2) | copy-done | bytes 1048600
  41.9 0.0 copy-start.4
  41.9 1.0 %all-to-all-done.1 = f32[32,8,128]{2,1,0:T(8,128)} async-done(((f32[32,8,128]{2,1,0:T(8,128)}), f32[32,8,128]{2,1,0:T(8,128)}, u32[]{:S(2)}, u32[]{:S(2)}) %all-to-all-start.1) | async-done | bytes 131104 | tf_op jit(solution)/shard_map/all_to_all | solution.py:256
  42.9 5.1 %all_gather.11.prefix = f32[4,128,128]{2,1,0:T(8,128)S(1)} all-gather(f32[2,128,128]{2,1,0:T(8,128)} %bitcast.2), channel_id=1, replica_groups=mesh['z'=8,'x'=4,'c'=2,'head'=8] {'c'}, dimensions={0}, use_global_device_ids=true | all-gather | bytes 393216 | tf_op jit(solution)/shard_map/all_gather | solution.py:257
  48.1 0.0 copy-start.3
  48.1 1.2 %copy-done.3 = bf16[1024,512]{1,0:T(8,128)(2,1)S(1)} copy-done((bf16[1024,512]{1,0:T(8,128)(2,1)S(1)}, bf16[1024,512]{1,0:T(8,128)(2,1)}, u32[]{:S(2)}) %copy-start.3) | copy-done | bytes 1048600
  49.3 1.8 %mix.1 = (f32[1024,512]{1,0:T(8,128)S(1)}, f32[8,8,128]{2,1,0:T(8,128)S(1)}) custom-call(f32[4,8,128]{2,1,0:T(8,128)S(1)} %get-tuple-element.11.wide, bf16[1024,512]{1,0:T(8,128)(2,1)S(1)} %copy-done.3, f32[1024,512]{1,0:T(8,128)S(1)} %get-tuple-element.14.local, f32[4,128,128]{2,1,0:T(8,128)S(1)} %all_gather.11.prefix), custom_call_target="tpu_custom_call" | custom-call | flops 268435456 | bytes 5242880 | tf_op jit(solution)/shard_map/mix/pallas_call | solution.py:273
  51.0 13.6 %all_to_all.16.squares = f32[8,8,128]{2,1,0:T(8,128)S(1)} all-to-all(f32[8,8,128]{2,1,0:T(8,128)S(1)} %get-tuple-element.16), channel_id=1, replica_groups=mesh['z'=8,'x'=4,'c'=2,'head'=8] {'head'}, dimensions={0} | all-to-all | bytes 65536 | tf_op jit(solution)/shard_map/all_to_all | solution.py:283
  64.6 0.0 copy-done.4
  64.6 1.1 %norm.1 = bf16[1024,512]{1,0:T(8,128)(2,1)} custom-call(f32[1024,512]{1,0:T(8,128)S(1)} %get-tuple-element.15.mixed, f32[8,8,128]{2,1,0:T(8,128)S(1)} %all_to_all.16.squares, f32[1,512]{1,0:T(1,128)S(1)} %bitcast.7), custom_call_target="tpu_custom_call" | custom-call | bytes 3145728 | tf_op jit(solution)/shard_map/norm/pallas_call | solution.py:284
  (1 shorter events, 0.0 us)
Async XLA Ops:
  0.0 0.7 copy-start.5
  29.0 13.9 %all-to-all-start.1 = ((f32[32,8,128]{2,1,0:T(8,128)}), f32[32,8,128]{2,1,0:T(8,128)}, u32[]{:S(2)}, u32[]{:S(2)}) async-start(f32[32,8,128]{2,1,0:T(8,128)} %scan.1), calls=%async_computation.1 | async-start | bytes 262144 | tf_op jit(solution)/shard_map/all_to_all | solution.py:256
  33.6 1.2 %copy-start = (bf16[1024,512]{1,0:T(8,128)(2,1)S(1)}, bf16[1024,512]{1,0:T(8,128)(2,1)}, u32[]{:S(2)}) copy-start(bf16[1024,512]{1,0:T(8,128)(2,1)} %keys_hbm.3) | copy-start | bytes 3145732
  34.8 1.2 %copy-start.1 = (bf16[1024,512]{1,0:T(8,128)(2,1)S(1)}, bf16[1024,512]{1,0:T(8,128)(2,1)}, u32[]{:S(2)}) copy-start(bf16[1024,512]{1,0:T(8,128)(2,1)} %values_hbm.3) | copy-start | bytes 3145732
  36.0 1.2 %copy-start.6 = (bf16[1024,512]{1,0:T(8,128)(2,1)S(1)}, bf16[1024,512]{1,0:T(8,128)(2,1)}, u32[]{:S(2)}) copy-start(bf16[1024,512]{1,0:T(8,128)(2,1)} %queries_hbm.1) | copy-start | bytes 3145732
  41.0 1.0 %copy-start.2 = (bf16[1024,512]{1,0:T(8,128)(2,1)}, bf16[1024,512]{1,0:T(8,128)(2,1)S(1)}, u32[]{:S(2)}) copy-start(bf16[1024,512]{1,0:T(8,128)(2,1)S(1)} %get-tuple-element.13.queries) | copy-start | bytes 3145732
  41.9 22.7 %copy-start.4 = (f32[512]{0:T(512)S(1)}, f32[512]{0:T(512)}, u32[]{:S(2)}) copy-start(f32[512]{0:T(512)} %param.9) | copy-start | bytes 6148
  48.1 1.2 %copy-start.3 = (bf16[1024,512]{1,0:T(8,128)(2,1)S(1)}, bf16[1024,512]{1,0:T(8,128)(2,1)}, u32[]{:S(2)}) copy-start(bf16[1024,512]{1,0:T(8,128)(2,1)} %copy-done.2) | copy-start | bytes 3145732

commit v3 on v2

--- a/solution.py
+++ b/solution.py
@@ -20,7 +20,9 @@
 BF16 = jnp.bfloat16
 VMEM_BYTES = 67043328
 STATES_ROOM = 11 << 20
-LOCAL_ROOM = 30 << 20
+LOCAL_ROOM = 3 << 20
+MIX_ROOM = 16 << 20
+SPARE = 8
 VMEM = pl.BlockSpec(memory_space=pltpu.VMEM)
 HBM = pl.BlockSpec(memory_space=pltpu.HBM)
 
@@ -106,72 +108,125 @@
     return jnp.concatenate([high, low], axis=0)
 
 
+def decay_mask(rate):
+    row = lax.broadcasted_iota(jnp.int32, (E, E), 0)
+    column = lax.broadcasted_iota(jnp.int32, (E, E), 1)
+    distance = (row - column).astype(F32)
+    within = jnp.where(distance >= 0, power(rate, jnp.maximum(distance, 0.0)), 0.0)
+    to_row = power(rate, row.astype(F32))
+    across = to_row * power(rate, (E - column[0:1]).astype(F32))
+    return within, across
+
+
 def local_kernel(
-    count, heads, wide, both, queries_hbm, keys_hbm, values_hbm, local, queries, keys, values, sems
+    count, heads, wide, both, queries_hbm, keys_hbm, values_hbm, local_hbm, staged_hbm,
+    local, queries, keys, values, held, scale, key_scale, within, across, rates, sems, out_sems, rate_sem,
 ):
     def copies(b):
         rows = pl.ds(b * BLOCK, BLOCK)
-        pairs = ((queries_hbm, queries), (keys_hbm, keys), (values_hbm, values))
+        pairs = ((keys_hbm, keys), (queries_hbm, queries), (values_hbm, values))
         return [
             pltpu.make_async_copy(source.at[rows], target.at[rows], sems.at[i, b])
             for i, (source, target) in enumerate(pairs)
         ]
 
+    def stores(b):
+        rows = pl.ds(b * BLOCK, BLOCK)
+        return [
+            pltpu.make_async_copy(local.at[rows], local_hbm.at[rows], out_sems.at[0, b]),
+            pltpu.make_async_copy(queries.at[rows], staged_hbm.at[rows], out_sems.at[1, b]),
+        ]
+
     for b in range(count):
         for copy in copies(b):
             copy.start()
     second = lax.axis_index("c") == 1
     inner = lax.broadcasted_iota(jnp.int32, (BLOCK, E), 0).astype(F32)
-    row = lax.broadcasted_iota(jnp.int32, (BLOCK, BLOCK), 0)
-    column = lax.broadcasted_iota(jnp.int32, (BLOCK, BLOCK), 1)
-    distance = (row - column).astype(F32)
-    for b in range(count):
+    for h in range(heads):
+        rates[:, head_columns(h)] = wide[h]
+    rate_copy = pltpu.make_async_copy(rates, local_hbm.at[pl.ds(count * BLOCK, 8)], rate_sem)
+    rate_copy.start()
+    for h in range(heads):
+        rate = wide[h, 0:1]
+        within[h], across[h] = decay_mask(rate)
+        scale[h] = power(rate, inner + 1.0)
+        key_scale[h] = power(rate, BLOCK - 1.0 - inner)
+        held[h] = jnp.where(second, both[0, h], 0.0)
+    top, bottom = slice(0, E), slice(E, BLOCK)
+    for b in range(count):
+        rows = pl.ds(b * BLOCK, BLOCK)
         for copy in copies(b):
             copy.wait()
-    for h in range(heads):
-        rate = jnp.concatenate([wide[h, 0:1]] * (BLOCK // E), axis=1)
-        masked = jnp.where(distance >= 0, power(rate, jnp.maximum(distance, 0.0)), 0.0)
-        scale = power(wide[h, 0:1], inner + 1.0)
-        key_scale = power(wide[h, 0:1], BLOCK - 1.0 - inner)
-        held = jnp.where(second, both[0, h], 0.0)
-        for b in range(count):
-            rows = pl.ds(b * BLOCK, BLOCK)
+        for h in range(heads):
             query = queries[rows, head_columns(h)]
+            key = keys[rows, head_columns(h)]
+            value = values[rows, head_columns(h)]
             scores = lax.dot_general(
-                query, keys[rows, head_columns(h)], (((1,), (1,)), ((), ())), preferred_element_type=F32
+                query, key, (((1,), (1,)), ((), ())), preferred_element_type=F32
             )
-            weights = (scores * masked).astype(BF16)
-            out = jnp.dot(weights, values[rows, head_columns(h)], preferred_element_type=F32)
+            upper = (scores[top, top] * within[h]).astype(BF16)
+            left = (scores[bottom, top] * across[h]).astype(BF16)
+            right = (scores[bottom, bottom] * within[h]).astype(BF16)
+            weights = jnp.concatenate(
+                [
+                    jnp.concatenate([upper, jnp.zeros((E, E), BF16)], axis=1),
+                    jnp.concatenate([left, right], axis=1),
+                ],
+                axis=0,
+            )
+            out = jnp.dot(weights, value, preferred_element_type=F32)
             doubled = jnp.concatenate([query, query], axis=1)
-            carried = jnp.dot(doubled, two_halves(held), preferred_element_type=F32)
-            local[rows, head_columns(h)] = out + carried * scale
+            carried = jnp.dot(doubled, two_halves(held[h]), preferred_element_type=F32)
+            local[rows, head_columns(h)] = out + carried * scale[h]
             if b < count - 1:
-                scaled = keys[rows, head_columns(h)].astype(F32) * key_scale
+                scaled = (key.astype(F32) * key_scale[h]).astype(BF16)
                 block = lax.dot_general(
-                    scaled.astype(BF16),
-                    values[rows, head_columns(h)],
-                    (((0,), (0,)), ((), ())),
-                    preferred_element_type=F32,
+                    scaled, value, (((0,), (0,)), ((), ())), preferred_element_type=F32
                 )
-                held = held * power(wide[h, 0:1], float(BLOCK)) + block
-
-
-def mix_kernel(count, heads, wide, queries, local, prefix, mixed, squares, scale):
+                held[h] = held[h] * power(wide[h, 0:1], float(BLOCK)) + block
+        for copy in stores(b):
+            copy.start()
+    for b in range(count):
+        for copy in stores(b):
+            copy.wait()
+    rate_copy.wait()
+
+
+def mix_kernel(
+    count, heads, queries_hbm, local_hbm, prefix, mixed, squares, scale, queries, local, rates, sems, rate_sem
+):
+    def copies(b):
+        rows = pl.ds(b * BLOCK, BLOCK)
+        return (
+            pltpu.make_async_copy(queries_hbm.at[rows], queries.at[rows], sems.at[0, b]),
+            pltpu.make_async_copy(local_hbm.at[rows], local.at[rows], sems.at[1, b]),
+        )
+
+    rate_copy = pltpu.make_async_copy(local_hbm.at[pl.ds(count * BLOCK, 8)], rates, rate_sem)
+    rate_copy.start()
+    for b in range(count):
+        for copy in copies(b):
+            copy.start()
     length = float(count * BLOCK)
     second = lax.axis_index("c") == 1
     inner = lax.broadcasted_iota(jnp.int32, (BLOCK, E), 0).astype(F32)
+    rate_copy.wait()
     entering = []
     for h in range(heads):
-        scale[h] = power(wide[h, 0:1], inner + 1.0)
-        entering.append(two_halves(prefix[h] * jnp.where(second, power(wide[h, 0:1], length), 1.0)))
-    for b in range(count):
-        rows = pl.ds(b * BLOCK, BLOCK)
+        rate = rates[0:1, head_columns(h)]
+        scale[h] = power(rate, inner + 1.0)
+        entering.append(two_halves(prefix[h] * jnp.where(second, power(rate, length), 1.0)))
+    for b in range(count):
+        rows = pl.ds(b * BLOCK, BLOCK)
+        for copy in copies(b):
+            copy.wait()
         total = jnp.zeros((BLOCK, E), F32)
         for h in range(heads):
             query = queries[rows, head_columns(h)]
             doubled = jnp.concatenate([query, query], axis=1)
             out = jnp.dot(doubled, entering[h], preferred_element_type=F32)
-            factor = scale[h] * power(wide[h, 0:1], float(b * BLOCK)) if b > 0 else scale[h]
+            decay = power(rates[0:1, head_columns(h)], float(b * BLOCK))
+            factor = scale[h] * decay if b > 0 else scale[h]
             out = local[rows, head_columns(h)] + out * factor
             mixed[rows, head_columns(h)] = out
             total = total + out * out
@@ -257,29 +312,47 @@
     prefix = lax.all_gather(mine, "c", tiled=True)
     local, staged = call(
         functools.partial(local_kernel, count, heads),
-        (shape((length, width), F32), shape((length, width), BF16)),
+        (shape((SPARE * length, width), F32), shape((SPARE * length, width), BF16)),
         [VMEM, VMEM, HBM, HBM, HBM],
-        (VMEM, VMEM),
+        (HBM, HBM),
         [
-            pltpu.VMEM((length, width), BF16),
-            pltpu.VMEM((length, width), BF16),
+            pltpu.VMEM((length, width), F32),
+            pltpu.VMEM((length, width), BF16),
+            pltpu.VMEM((length, width), BF16),
+            pltpu.VMEM((length, width), BF16),
+            pltpu.VMEM((heads, E, E), F32),
+            pltpu.VMEM((heads, BLOCK, E), F32),
+            pltpu.VMEM((heads, BLOCK, E), F32),
+            pltpu.VMEM((heads, E, E), F32),
+            pltpu.VMEM((heads, E, E), F32),
+            pltpu.VMEM((8, width), F32),
             pltpu.SemaphoreType.DMA((3, count)),
+            pltpu.SemaphoreType.DMA((2, count)),
+            pltpu.SemaphoreType.DMA,
         ],
         room=LOCAL_ROOM,
-        flops=1 << 40,
-        moved=0,
+        flops=8 * length * BLOCK * width,
+        moved=12 * length * width,
         name="local",
     )(wide, both, queries, key_rows, value_rows)
     mixed, squares = call(
         functools.partial(mix_kernel, count, heads),
         (shape((length, width), F32), shape((parts, length // E, E), F32)),
-        [VMEM] * 4,
+        [HBM, HBM, VMEM],
         (VMEM, VMEM),
-        [pltpu.VMEM((heads, BLOCK, E), F32)],
+        [
+            pltpu.VMEM((heads, BLOCK, E), F32),
+            pltpu.VMEM((length, width), BF16),
+            pltpu.VMEM((length, width), F32),
+            pltpu.VMEM((8, width), F32),
+            pltpu.SemaphoreType.DMA((2, count)),
+            pltpu.SemaphoreType.DMA,
+        ],
+        room=MIX_ROOM,
         flops=4 * length * E * width,
         moved=10 * length * width,
         name="mix",
-    )(wide, staged, local, prefix)
+    )(staged, local, prefix)
     shared = lax.all_to_all(squares, HEAD, 0, 0, tiled=True)
     return call(
         functools.partial(norm_kernel, count),

time: 66.2 us -> 66.7 us (level)
  local copies, waits for them, and re-layouts: 6.52 us -> 0.67 us
  Pallas kernels: 9.61 us -> 14.8 us
  waiting for transfers between devices: 0.99 us -> 3.11 us
  starting transfers between devices: 4.56 us -> 3.88 us
    unnamed x14 -> x8, local copies, waits for them, and re-layouts: 6.52 us -> 0.67 us
    pallas_call x1, Pallas kernels: 1.76 us -> 4.4 us  [body(): call(functools.partial(mix_kernel, count, heads), (shape((length, width),...]
    pallas_call x1, Pallas kernels: 3.73 us -> 6.21 us  [body(): call(functools.partial(local_kernel, count, heads), (shape((SPARE * lengt...]
    all_to_all x1, waiting for transfers between devices: 0.99 us -> 3.11 us  [body(): mine = lax.all_to_all(prefixes, CHIPS, 0, 0, tiled=True).reshape(half, E, E)]
    all_to_all x1, starting transfers between devices: 4.56 us -> 3.88 us  [body(): mine = lax.all_to_all(prefixes, CHIPS, 0, 0, tiled=True).reshape(half, E, E)]
  transfers between devices with their start and end apart: 1 -> 1, of which waited for: 1 -> 1; matrix products, arithmetic and copies ran while one was open for 0% -> 0% of each run, Pallas kernels for 6% -> 9%
where the time goes in v3:
time: 66.7 us; the launch traced here: 66.3 us
  blocking collectives  43.8 us (66%)
  Pallas kernels  14.8 us (22%)
  starting transfers between devices  3.88 us (6%)
  waiting for transfers between devices  3.11 us (5%)
  local copies, waits for them, and re-layouts  0.67 us (1%)
    all_to_all x1, blocking collectives, body(): owned = lax.all_to_all(total.reshape(chips, -1, E), CHIPS, 0, 0, tiled=True)  16.7 us
    all_to_all x1, blocking collectives, body(): shared = lax.all_to_all(squares, HEAD, 0, 0, tiled=True)  13.6 us
    all_gather x1, blocking collectives, body(): both = lax.all_gather(state, 'c')  8.65 us
    pallas_call x1, Pallas kernels, body(): call(functools.partial(local_kernel, count, heads), (shape((SPARE * lengt...  6.21 us
    all_gather x1, blocking collectives, body(): prefix = lax.all_gather(mine, 'c', tiled=True)  4.94 us
    pallas_call x1, Pallas kernels, body(): call(functools.partial(mix_kernel, count, heads), (shape((length, width),...  4.4 us
    all_to_all x1, starting transfers between devices, body(): mine = lax.all_to_all(prefixes, CHIPS, 0, 0, tiled=True).reshape(half, E, E)  3.88 us
    all_to_all x1, waiting for transfers between devices, body(): mine = lax.all_to_all(prefixes, CHIPS, 0, 0, tiled=True).reshape(half, E, E)  3.11 us
  transfers between devices with their start and end apart: 1, of which 1 were waited for; matrix products, arithmetic and copies ran while one was open for 0% of the time, Pallas kernels for 9%

profile of v3, /device:TPU:1, one launch (start us, length us, event | category | flops | bytes accessed | tf_op | source)
XLA Modules:
  0.0 66.3 jit_solution(17829351700371829027)
XLA Ops:
  0.0 0.0 copy-start.3
  0.0 0.7 copy-done.3
  0.7 2.2 %states.1 = (f32[4,128,128]{2,1,0:T(8,128)S(1)}, f32[4,8,128]{2,1,0:T(8,128)S(1)}) custom-call(f32[4]{0:T(128)S(1)} %copy-done.3, bf16[1024,512]{1,0:T(8,128)(2,1)} %keys_hbm.3, bf16[1024,512]{1,0:T(8,128)(2,1)} %values_hbm.3), custom_call_target="tpu_custom_call" | custom-call | flops 134217728 | bytes 2097152 | tf_op jit(solution)/shard_map/states/pallas_call | solution.py:274
  2.9 0.0 copy-start.1
  2.9 8.6 %all-gather = f32[8,128,128]{2,1,0:T(8,128)S(1)} all-gather(f32[4,128,128]{2,1,0:T(8,128)S(1)} %get-tuple-element.12), channel_id=2, replica_groups=mesh['z'=8,'x'=4,'c'=2,'head'=8] {'c'}, dimensions={0}, use_global_device_ids=true | all-gather | bytes 786432 | tf_op jit(solution)/shard_map/all_gather | solution.py:295
  11.6 0.0 copy-start
  11.6 16.7 %all_to_all.15.totals = f32[32,8,128]{2,1,0:T(8,128)S(1)} all-to-all(f32[32,8,128]{2,1,0:T(8,128)S(1)} %bitcast.6), channel_id=1, replica_groups=mesh['z'=8,'x'=4,'c'=2,'head'=8] {'z','x'}, dimensions={0} | all-to-all | bytes 262144 | tf_op jit(solution)/shard_map/all_to_all | solution.py:303
  28.3 0.8 %scan.1 = f32[32,8,128]{2,1,0:T(8,128)} custom-call(f32[4,8,128]{2,1,0:T(8,128)S(1)} %get-tuple-element.11.wide, f32[32,8,128]{2,1,0:T(8,128)S(1)} %all_to_all.15.totals), custom_call_target="tpu_custom_call" | custom-call | tf_op jit(solution)/shard_map/scan/pallas_call | solution.py:304
  29.0 3.9 %all-to-all-start.1 = ((f32[32,8,128]{2,1,0:T(8,128)}), f32[32,8,128]{2,1,0:T(8,128)S(1)}, u32[]{:S(2)}, u32[]{:S(2)}) async-start(f32[32,8,128]{2,1,0:T(8,128)} %scan.1), calls=%async_computation.1 | async-start | bytes 262144 | tf_op jit(solution)/shard_map/all_to_all | solution.py:311
  32.9 0.0 copy-done.1
  32.9 0.0 copy-done
  32.9 6.2 %local.1 = (f32[8192,512]{1,0:T(8,128)}, bf16[8192,512]{1,0:T(8,128)(2,1)}) custom-call(f32[4,8,128]{2,1,0:T(8,128)} %copy-done.1, f32[2,4,128,128]{3,2,1,0:T(8,128)} %bitcast.5, bf16[1024,512]{1,0:T(8,128)(2,1)} %queries_hbm.1, bf16[1024,512]{1,0:T(8,128)(2,1)} %keys_hbm.3, bf16[1024,512]{1,0:T(8,128)(2,1)} %values_hbm.3), custom_call_target="tpu_custom_call" | custom-call | flops 1073741824 | bytes 6291456 | tf_op jit(solution)/shard_map/local/pallas_call | solution.py:313
  39.1 3.1 %all-to-all-done.1 = f32[32,8,128]{2,1,0:T(8,128)S(1)} async-done(((f32[32,8,128]{2,1,0:T(8,128)}), f32[32,8,128]{2,1,0:T(8,128)S(1)}, u32[]{:S(2)}, u32[]{:S(2)}) %all-to-all-start.1) | async-done | bytes 131104 | tf_op jit(solution)/shard_map/all_to_all | solution.py:311
  42.3 4.9 %all_gather.11.prefix = f32[4,128,128]{2,1,0:T(8,128)S(1)} all-gather(f32[2,128,128]{2,1,0:T(8,128)S(1)} %bitcast.8), channel_id=1, replica_groups=mesh['z'=8,'x'=4,'c'=2,'head'=8] {'c'}, dimensions={0}, use_global_device_ids=true | all-gather | bytes 393216 | tf_op jit(solution)/shard_map/all_gather | solution.py:312
  47.2 0.0 copy-start.2
  47.2 4.4 %mix.1 = (f32[1024,512]{1,0:T(8,128)S(1)}, f32[8,8,128]{2,1,0:T(8,128)S(1)}) custom-call(bf16[8192,512]{1,0:T(8,128)(2,1)} %get-tuple-element.13.queries_hbm, f32[8192,512]{1,0:T(8,128)} %get-tuple-element.14.local_hbm, f32[4,128,128]{2,1,0:T(8,128)S(1)} %all_gather.11.prefix), custom_call_target="tpu_custom_call" | custom-call | flops 268435456 | bytes 5242880 | tf_op jit(solution)/shard_map/mix/pallas_call | solution.py:338
  51.6 13.6 %all_to_all.16.squares = f32[8,8,128]{2,1,0:T(8,128)S(1)} all-to-all(f32[8,8,128]{2,1,0:T(8,128)S(1)} %get-tuple-element.16), channel_id=1, replica_groups=mesh['z'=8,'x'=4,'c'=2,'head'=8] {'head'}, dimensions={0} | all-to-all | bytes 65536 | tf_op jit(solution)/shard_map/all_to_all | solution.py:356
  65.2 0.0 copy-done.2
  65.2 1.1 %norm.1 = bf16[1024,512]{1,0:T(8,128)(2,1)} custom-call(f32[1024,512]{1,0:T(8,128)S(1)} %get-tuple-element.15.mixed, f32[8,8,128]{2,1,0:T(8,128)S(1)} %all_to_all.16.squares, f32[1,512]{1,0:T(1,128)S(1)} %bitcast.7), custom_call_target="tpu_custom_call" | custom-call | bytes 3145728 | tf_op jit(solution)/shard_map/norm/pallas_call | solution.py:357
  (1 shorter events, 0.0 us)
Async XLA Ops:
  0.0 0.7 copy-start.3
  2.9 30.0 %copy-start.1 = (f32[4,8,128]{2,1,0:T(8,128)}, f32[4,8,128]{2,1,0:T(8,128)S(1)}, u32[]{:S(2)}) copy-start(f32[4,8,128]{2,1,0:T(8,128)S(1)} %get-tuple-element.11.wide) | copy-start | bytes 49156
  11.6 21.4 %copy-start = (f32[8,128,128]{2,1,0:T(8,128)}, f32[8,128,128]{2,1,0:T(8,128)S(1)}, u32[]{:S(2)}) copy-start(f32[8,128,128]{2,1,0:T(8,128)S(1)} %all-gather) | copy-start | bytes 1572868
  29.0 13.2 %all-to-all-start.1 = ((f32[32,8,128]{2,1,0:T(8,128)}), f32[32,8,128]{2,1,0:T(8,128)S(1)}, u32[]{:S(2)}, u32[]{:S(2)}) async-start(f32[32,8,128]{2,1,0:T(8,128)} %scan.1), calls=%async_computation.1 | async-start | bytes 262144 | tf_op jit(solution)/shard_map/all_to_all | solution.py:311
  47.2 18.0 %copy-start.2 = (f32[512]{0:T(512)S(1)}, f32[512]{0:T(512)}, u32[]{:S(2)}) copy-start(f32[512]{0:T(512)} %param.9) | copy-start | bytes 6148

commit v4 on v3

--- a/solution.py
+++ b/solution.py
@@ -20,9 +20,10 @@
 BF16 = jnp.bfloat16
 VMEM_BYTES = 67043328
 STATES_ROOM = 11 << 20
-LOCAL_ROOM = 3 << 20
-MIX_ROOM = 16 << 20
-SPARE = 8
+LOCAL_ROOM = 40 << 20
+ROWS = 128
+DECAY_FLOPS = 1 << 30
+DECAY_MOVED = 8 << 20
 VMEM = pl.BlockSpec(memory_space=pltpu.VMEM)
 HBM = pl.BlockSpec(memory_space=pltpu.HBM)
 
@@ -118,45 +119,24 @@
     return within, across
 
 
-def local_kernel(
-    count, heads, wide, both, queries_hbm, keys_hbm, values_hbm, local_hbm, staged_hbm,
-    local, queries, keys, values, held, scale, key_scale, within, across, rates, sems, out_sems, rate_sem,
-):
-    def copies(b):
-        rows = pl.ds(b * BLOCK, BLOCK)
-        pairs = ((keys_hbm, keys), (queries_hbm, queries), (values_hbm, values))
-        return [
-            pltpu.make_async_copy(source.at[rows], target.at[rows], sems.at[i, b])
-            for i, (source, target) in enumerate(pairs)
-        ]
-
-    def stores(b):
-        rows = pl.ds(b * BLOCK, BLOCK)
-        return [
-            pltpu.make_async_copy(local.at[rows], local_hbm.at[rows], out_sems.at[0, b]),
-            pltpu.make_async_copy(queries.at[rows], staged_hbm.at[rows], out_sems.at[1, b]),
-        ]
-
-    for b in range(count):
-        for copy in copies(b):
-            copy.start()
-    second = lax.axis_index("c") == 1
+def decay_kernel(heads, wide, within, across, scale, key_scale):
     inner = lax.broadcasted_iota(jnp.int32, (BLOCK, E), 0).astype(F32)
-    for h in range(heads):
-        rates[:, head_columns(h)] = wide[h]
-    rate_copy = pltpu.make_async_copy(rates, local_hbm.at[pl.ds(count * BLOCK, 8)], rate_sem)
-    rate_copy.start()
     for h in range(heads):
         rate = wide[h, 0:1]
         within[h], across[h] = decay_mask(rate)
         scale[h] = power(rate, inner + 1.0)
         key_scale[h] = power(rate, BLOCK - 1.0 - inner)
+
+
+def local_kernel(
+    count, heads, wide, within, across, scale, key_scale, both, queries, keys, values, local, held
+):
+    second = lax.axis_index("c") == 1
+    for h in range(heads):
         held[h] = jnp.where(second, both[0, h], 0.0)
     top, bottom = slice(0, E), slice(E, BLOCK)
     for b in range(count):
         rows = pl.ds(b * BLOCK, BLOCK)
-        for copy in copies(b):
-            copy.wait()
         for h in range(heads):
             query = queries[rows, head_columns(h)]
             key = keys[rows, head_columns(h)]
@@ -184,62 +164,36 @@
                     scaled, value, (((0,), (0,)), ((), ())), preferred_element_type=F32
                 )
                 held[h] = held[h] * power(wide[h, 0:1], float(BLOCK)) + block
-        for copy in stores(b):
-            copy.start()
-    for b in range(count):
-        for copy in stores(b):
-            copy.wait()
-    rate_copy.wait()
-
-
-def mix_kernel(
-    count, heads, queries_hbm, local_hbm, prefix, mixed, squares, scale, queries, local, rates, sems, rate_sem
-):
-    def copies(b):
-        rows = pl.ds(b * BLOCK, BLOCK)
-        return (
-            pltpu.make_async_copy(queries_hbm.at[rows], queries.at[rows], sems.at[0, b]),
-            pltpu.make_async_copy(local_hbm.at[rows], local.at[rows], sems.at[1, b]),
-        )
-
-    rate_copy = pltpu.make_async_copy(local_hbm.at[pl.ds(count * BLOCK, 8)], rates, rate_sem)
-    rate_copy.start()
-    for b in range(count):
-        for copy in copies(b):
-            copy.start()
+
+
+def relay_kernel(mine, prefix):
+    prefix[...] = mine[...]
+
+
+def mix_kernel(count, heads, wide, scale, queries, local, prefix, mixed, squares):
     length = float(count * BLOCK)
     second = lax.axis_index("c") == 1
-    inner = lax.broadcasted_iota(jnp.int32, (BLOCK, E), 0).astype(F32)
-    rate_copy.wait()
     entering = []
     for h in range(heads):
-        rate = rates[0:1, head_columns(h)]
-        scale[h] = power(rate, inner + 1.0)
-        entering.append(two_halves(prefix[h] * jnp.where(second, power(rate, length), 1.0)))
-    for b in range(count):
-        rows = pl.ds(b * BLOCK, BLOCK)
-        for copy in copies(b):
-            copy.wait()
-        total = jnp.zeros((BLOCK, E), F32)
+        entering.append(two_halves(prefix[h] * jnp.where(second, power(wide[h, 0:1], length), 1.0)))
+    for t in range(count * BLOCK // ROWS):
+        rows = pl.ds(t * ROWS, ROWS)
+        inner = t * ROWS % BLOCK
+        block = t * ROWS // BLOCK
+        total = jnp.zeros((ROWS, E), F32)
         for h in range(heads):
             query = queries[rows, head_columns(h)]
             doubled = jnp.concatenate([query, query], axis=1)
             out = jnp.dot(doubled, entering[h], preferred_element_type=F32)
-            decay = power(rates[0:1, head_columns(h)], float(b * BLOCK))
-            factor = scale[h] * decay if b > 0 else scale[h]
+            factor = scale[h, inner : inner + ROWS]
+            if block > 0:
+                factor = factor * power(wide[h, 0:1], float(block * BLOCK))
             out = local[rows, head_columns(h)] + out * factor
             mixed[rows, head_columns(h)] = out
             total = total + out * out
-        sums = lax.dot_general(
-            jnp.ones((8, E), F32),
-            total,
-            (((1,), (1,)), ((), ())),
-            precision=lax.Precision.HIGHEST,
-            preferred_element_type=F32,
-        )
-        for r in range(BLOCK // E):
-            row = jnp.broadcast_to(sums[0:1, r * E : (r + 1) * E], (squares.shape[0], E))
-            squares[:, b * (BLOCK // E) + r, :] = row
+        for r in range(ROWS // E):
+            sums = jnp.sum(total[r * E : (r + 1) * E].T, axis=0, keepdims=True)
+            squares[:, t * (ROWS // E) + r, :] = jnp.broadcast_to(sums, (squares.shape[0], E))
 
 
 def norm_kernel(count, mixed, squares, gain, out_hbm, out, sems):
@@ -309,50 +263,50 @@
         name="scan",
     )(wide, owned)
     mine = lax.all_to_all(prefixes, CHIPS, 0, 0, tiled=True).reshape(half, E, E)
+    mine = call(
+        relay_kernel,
+        shape(mine.shape, F32),
+        [VMEM],
+        VMEM,
+        flops=DECAY_FLOPS,
+        moved=DECAY_MOVED,
+        name="relay",
+    )(mine)
     prefix = lax.all_gather(mine, "c", tiled=True)
-    local, staged = call(
+    decays = call(
+        functools.partial(decay_kernel, heads),
+        (
+            shape((heads, E, E), F32),
+            shape((heads, E, E), F32),
+            shape((heads, BLOCK, E), F32),
+            shape((heads, BLOCK, E), F32),
+        ),
+        [VMEM],
+        (VMEM,) * 4,
+        flops=DECAY_FLOPS,
+        moved=DECAY_MOVED,
+        name="decays",
+    )(wide)
+    local = call(
         functools.partial(local_kernel, count, heads),
-        (shape((SPARE * length, width), F32), shape((SPARE * length, width), BF16)),
-        [VMEM, VMEM, HBM, HBM, HBM],
-        (HBM, HBM),
-        [
-            pltpu.VMEM((length, width), F32),
-            pltpu.VMEM((length, width), BF16),
-            pltpu.VMEM((length, width), BF16),
-            pltpu.VMEM((length, width), BF16),
-            pltpu.VMEM((heads, E, E), F32),
-            pltpu.VMEM((heads, BLOCK, E), F32),
-            pltpu.VMEM((heads, BLOCK, E), F32),
-            pltpu.VMEM((heads, E, E), F32),
-            pltpu.VMEM((heads, E, E), F32),
-            pltpu.VMEM((8, width), F32),
-            pltpu.SemaphoreType.DMA((3, count)),
-            pltpu.SemaphoreType.DMA((2, count)),
-            pltpu.SemaphoreType.DMA,
-        ],
+        shape((length, width), F32),
+        [VMEM] * 9,
+        VMEM,
+        [pltpu.VMEM((heads, E, E), F32)],
         room=LOCAL_ROOM,
         flops=8 * length * BLOCK * width,
-        moved=12 * length * width,
+        moved=10 * length * width,
         name="local",
-    )(wide, both, queries, key_rows, value_rows)
+    )(wide, *decays, both, queries, key_rows, value_rows)
     mixed, squares = call(
         functools.partial(mix_kernel, count, heads),
         (shape((length, width), F32), shape((parts, length // E, E), F32)),
-        [HBM, HBM, VMEM],
+        [VMEM] * 5,
         (VMEM, VMEM),
-        [
-            pltpu.VMEM((heads, BLOCK, E), F32),
-            pltpu.VMEM((length, width), BF16),
-            pltpu.VMEM((length, width), F32),
-            pltpu.VMEM((8, width), F32),
-            pltpu.SemaphoreType.DMA((2, count)),
-            pltpu.SemaphoreType.DMA,
-        ],
-        room=MIX_ROOM,
         flops=4 * length * E * width,
         moved=10 * length * width,
         name="mix",
-    )(staged, local, prefix)
+    )(wide, decays[2], queries, local, prefix)
     shared = lax.all_to_all(squares, HEAD, 0, 0, tiled=True)
     return call(
         functools.partial(norm_kernel, count),

time: 66.7 us -> 63.1 us (0.946)
  Pallas kernels: 14.8 us -> 7.62 us
  waiting for transfers between devices: 3.11 us -> 5.02 us
  local copies, waits for them, and re-layouts: 0.67 us -> 2.26 us
    pallas_call x1, Pallas kernels: 4.4 us -> 0.79 us  [body(): call(functools.partial(mix_kernel, count, heads), (shape((length, width),...]
    pallas_call x1 -> x3, Pallas kernels: 6.21 us -> 2.7 us  [the longest x1 2.46 us: body(): call(functools.partial(local_kernel, count, heads), shape((length, width)...]
    all_to_all x1, waiting for transfers between devices: 3.11 us -> 5.02 us  [body(): mine = lax.all_to_all(prefixes, CHIPS, 0, 0, tiled=True).reshape(half, E, E)]
    unnamed x8 -> x12, local copies, waits for them, and re-layouts: 0.67 us -> 2.26 us
  transfers between devices with their start and end apart: 1 -> 1, of which waited for: 1 -> 1; matrix products, arithmetic and copies ran while one was open for 0% -> 0% of each run, Pallas kernels for 9% -> 4%
where the time goes in v4:
time: 63.1 us; the launch traced here: 62.8 us
  blocking collectives  44 us (70%)
  Pallas kernels  7.62 us (12%)
  waiting for transfers between devices  5.02 us (8%)
  starting transfers between devices  3.87 us (6%)
  local copies, waits for them, and re-layouts  2.26 us (4%)
    all_to_all x1, blocking collectives, body(): owned = lax.all_to_all(total.reshape(chips, -1, E), CHIPS, 0, 0, tiled=True)  16.7 us
    all_to_all x1, blocking collectives, body(): shared = lax.all_to_all(squares, HEAD, 0, 0, tiled=True)  13.6 us
    all_gather x1, blocking collectives, body(): both = lax.all_gather(state, 'c')  8.65 us
    all_gather x1, blocking collectives, body(): prefix = lax.all_gather(mine, 'c', tiled=True)  5.09 us
    all_to_all x1, waiting for transfers between devices, body(): mine = lax.all_to_all(prefixes, CHIPS, 0, 0, tiled=True).reshape(half, E, E)  5.02 us
    all_to_all x1, starting transfers between devices, body(): mine = lax.all_to_all(prefixes, CHIPS, 0, 0, tiled=True).reshape(half, E, E)  3.87 us
    pallas_call x1, Pallas kernels, body(): call(functools.partial(local_kernel, count, heads), shape((length, width)...  2.46 us
    unnamed x12, local copies, waits for them, and re-layouts  2.26 us
  transfers between devices with their start and end apart: 1, of which 1 were waited for; matrix products, arithmetic and copies ran while one was open for 0% of the time, Pallas kernels for 4%

profile of v4, /device:TPU:1, one launch (start us, length us, event | category | flops | bytes accessed | tf_op | source)
XLA Modules:
  0.0 62.8 jit_solution(9523910468337193321)
XLA Ops:
  0.0 0.0 copy-start.5
  0.0 0.7 %copy-done.5 = f32[4]{0:T(128)S(1)} copy-done((f32[4]{0:T(128)S(1)}, f32[4]{0:T(128)}, u32[]{:S(2)}) %copy-start.5) | copy-done | bytes 40
  0.7 2.2 %states.1 = (f32[4,128,128]{2,1,0:T(8,128)S(1)}, f32[4,8,128]{2,1,0:T(8,128)S(1)}) custom-call(f32[4]{0:T(128)S(1)} %copy-done.5, bf16[1024,512]{1,0:T(8,128)(2,1)} %keys.1, bf16[1024,512]{1,0:T(8,128)(2,1)} %values.1), custom_call_target="tpu_custom_call" | custom-call | flops 134217728 | bytes 2097152 | tf_op jit(solution)/shard_map/states/pallas_call | solution.py:228
  2.9 8.6 %all-gather = f32[8,128,128]{2,1,0:T(8,128)S(1)} all-gather(f32[4,128,128]{2,1,0:T(8,128)S(1)} %get-tuple-element.18), channel_id=2, replica_groups=mesh['z'=8,'x'=4,'c'=2,'head'=8] {'c'}, dimensions={0}, use_global_device_ids=true | all-gather | bytes 786432 | tf_op jit(solution)/shard_map/all_gather | solution.py:249
  11.6 16.7 %all_to_all.15.totals = f32[32,8,128]{2,1,0:T(8,128)S(1)} all-to-all(f32[32,8,128]{2,1,0:T(8,128)S(1)} %bitcast.6), channel_id=1, replica_groups=mesh['z'=8,'x'=4,'c'=2,'head'=8] {'z','x'}, dimensions={0} | all-to-all | bytes 262144 | tf_op jit(solution)/shard_map/all_to_all | solution.py:257
  28.3 0.7 %scan.1 = f32[32,8,128]{2,1,0:T(8,128)} custom-call(f32[4,8,128]{2,1,0:T(8,128)S(1)} %get-tuple-element.13.wide, f32[32,8,128]{2,1,0:T(8,128)S(1)} %all_to_all.15.totals), custom_call_target="tpu_custom_call" | custom-call | tf_op jit(solution)/shard_map/scan/pallas_call | solution.py:258
  29.0 3.9 %all-to-all-start.1 = ((f32[32,8,128]{2,1,0:T(8,128)}), f32[32,8,128]{2,1,0:T(8,128)S(1)}, u32[]{:S(2)}, u32[]{:S(2)}) async-start(f32[32,8,128]{2,1,0:T(8,128)} %scan.1), calls=%async_computation.1 | async-start | bytes 262144 | tf_op jit(solution)/shard_map/all_to_all | solution.py:265
  32.9 0.0 copy-start
  32.9 0.0 copy-start.1
  32.9 0.0 copy-start.2
  32.9 0.2 decays.1
  33.2 0.9 %copy-done = bf16[1024,512]{1,0:T(8,128)(2,1)S(1)} copy-done((bf16[1024,512]{1,0:T(8,128)(2,1)S(1)}, bf16[1024,512]{1,0:T(8,128)(2,1)}, u32[]{:S(2)}) %copy-start) | copy-done | bytes 1048600
  34.1 0.3 copy-done.1
  34.4 0.3 copy-done.2
  34.7 2.5 %local.1 = f32[1024,512]{1,0:T(8,128)S(1)} custom-call(f32[4,8,128]{2,1,0:T(8,128)S(1)} %get-tuple-element.13.wide, f32[4,128,128]{2,1,0:T(8,128)S(1)} %get-tuple-element.15.within, f32[4,128,128]{2,1,0:T(8,128)S(1)} %get-tuple-element.16.across, f32[4,256,128]{2,1,0:T(8,128)S(1)} %get-tuple-element.14.scale, ...), custom_call_target="tpu_custom_call" | custom-call | flops 1073741824 | bytes 5242880 | tf_op jit(solution)/shard_map/local/pallas_call | solution.py:290
  37.2 5.0 %all-to-all-done.1 = f32[32,8,128]{2,1,0:T(8,128)S(1)} async-done(((f32[32,8,128]{2,1,0:T(8,128)}), f32[32,8,128]{2,1,0:T(8,128)S(1)}, u32[]{:S(2)}, u32[]{:S(2)}) %all-to-all-start.1) | async-done | bytes 131104 | tf_op jit(solution)/shard_map/all_to_all | solution.py:265
  42.2 0.0 copy-start.3
  42.2 5.1 %all_gather.11.prefix = f32[4,128,128]{2,1,0:T(8,128)S(1)} all-gather(f32[2,128,128]{2,1,0:T(8,128)S(1)} %relay.1), channel_id=1, replica_groups=mesh['z'=8,'x'=4,'c'=2,'head'=8] {'c'}, dimensions={0}, use_global_device_ids=true | all-gather | bytes 393216 | tf_op jit(solution)/shard_map/all_gather | solution.py:275
  47.3 0.0 copy-done.3
  47.3 0.0 copy-start.4
  47.3 0.8 %mix.1 = (f32[1024,512]{1,0:T(8,128)S(1)}, f32[8,8,128]{2,1,0:T(8,128)S(1)}) custom-call(f32[4,8,128]{2,1,0:T(8,128)S(1)} %get-tuple-element.13.wide, f32[4,256,128]{2,1,0:T(8,128)S(1)} %get-tuple-element.14.scale, bf16[1024,512]{1,0:T(8,128)(2,1)S(1)} %copy-done.3, f32[1024,512]{1,0:T(8,128)S(1)} %local.1, f32[4,128,128]{2,1,0:T(8,128)S(1)} %all_gather.11.prefix), custom_call_target="tpu_custom_call" | custom-call | flops 268435456 | bytes 5242880 | tf_op jit(solution)/shard_map/mix/pallas_call | solution.py:301
  48.1 13.6 %all_to_all.16.squares = f32[8,8,128]{2,1,0:T(8,128)S(1)} all-to-all(f32[8,8,128]{2,1,0:T(8,128)S(1)} %get-tuple-element.20), channel_id=1, replica_groups=mesh['z'=8,'x'=4,'c'=2,'head'=8] {'head'}, dimensions={0} | all-to-all | bytes 65536 | tf_op jit(solution)/shard_map/all_to_all | solution.py:310
  61.7 0.0 copy-done.4
  61.7 1.1 %norm.1 = bf16[1024,512]{1,0:T(8,128)(2,1)} custom-call(f32[1024,512]{1,0:T(8,128)S(1)} %get-tuple-element.19.mixed, f32[8,8,128]{2,1,0:T(8,128)S(1)} %all_to_all.16.squares, f32[1,512]{1,0:T(1,128)S(1)} %bitcast.8), custom_call_target="tpu_custom_call" | custom-call | bytes 3145728 | tf_op jit(solution)/shard_map/norm/pallas_call | solution.py:311
  (2 shorter events, 0.0 us)
Async XLA Ops:
  0.0 0.7 %copy-start.5 = (f32[4]{0:T(128)S(1)}, f32[4]{0:T(128)}, u32[]{:S(2)}) copy-start(f32[4]{0:T(128)} %rates_hbm.1) | copy-start | bytes 52
  29.0 13.2 %all-to-all-start.1 = ((f32[32,8,128]{2,1,0:T(8,128)}), f32[32,8,128]{2,1,0:T(8,128)S(1)}, u32[]{:S(2)}, u32[]{:S(2)}) async-start(f32[32,8,128]{2,1,0:T(8,128)} %scan.1), calls=%async_computation.1 | async-start | bytes 262144 | tf_op jit(solution)/shard_map/all_to_all | solution.py:265
  32.9 1.2 %copy-start = (bf16[1024,512]{1,0:T(8,128)(2,1)S(1)}, bf16[1024,512]{1,0:T(8,128)(2,1)}, u32[]{:S(2)}) copy-start(bf16[1024,512]{1,0:T(8,128)(2,1)} %keys.1) | copy-start | bytes 3145732
  32.9 1.5 %copy-start.1 = (bf16[1024,512]{1,0:T(8,128)(2,1)S(1)}, bf16[1024,512]{1,0:T(8,128)(2,1)}, u32[]{:S(2)}) copy-start(bf16[1024,512]{1,0:T(8,128)(2,1)} %values.1) | copy-start | bytes 3145732
  32.9 1.8 %copy-start.2 = (bf16[1024,512]{1,0:T(8,128)(2,1)S(1)}, bf16[1024,512]{1,0:T(8,128)(2,1)}, u32[]{:S(2)}) copy-start(bf16[1024,512]{1,0:T(8,128)(2,1)} %queries.3) | copy-start | bytes 3145732
  42.2 5.1 %copy-start.3 = (bf16[1024,512]{1,0:T(8,128)(2,1)S(1)}, bf16[1024,512]{1,0:T(8,128)(2,1)}, u32[]{:S(2)}) copy-start(bf16[1024,512]{1,0:T(8,128)(2,1)} %queries.3) | copy-start | bytes 3145732
  47.3 14.4 %copy-start.4 = (f32[512]{0:T(512)S(1)}, f32[512]{0:T(512)}, u32[]{:S(2)}) copy-start(f32[512]{0:T(512)} %param.9) | copy-start | bytes 6148

commit v5 on v4

--- a/solution.py
+++ b/solution.py
@@ -19,7 +19,6 @@
 F32 = jnp.float32
 BF16 = jnp.bfloat16
 VMEM_BYTES = 67043328
-STATES_ROOM = 11 << 20
 LOCAL_ROOM = 40 << 20
 ROWS = 128
 DECAY_FLOPS = 1 << 30
@@ -49,41 +48,28 @@
     return slice(h * E, (h + 1) * E)
 
 
-def states_kernel(
-    count, heads, rates_hbm, keys_hbm, values_hbm, state, wide, keys, values, scale, rates, sems, rate_sem
-):
-    def copies(b):
-        rows = pl.ds(b * BLOCK, BLOCK)
-        return (
-            pltpu.make_async_copy(keys_hbm.at[rows], keys.at[rows], sems.at[0, b]),
-            pltpu.make_async_copy(values_hbm.at[rows], values.at[rows], sems.at[1, b]),
-        )
-
-    rate_copy = pltpu.make_async_copy(rates_hbm, rates, rate_sem)
-    rate_copy.start()
-    for b in range(count):
-        for copy in copies(b):
-            copy.start()
-    inner = lax.broadcasted_iota(jnp.int32, (BLOCK, E), 0).astype(F32)
-    rate_copy.wait()
+def positions_kernel(inner):
+    inner[...] = lax.broadcasted_iota(jnp.int32, inner.shape, 0).astype(F32)
+
+
+def states_kernel(count, heads, inner, rates, keys, values, state, wide):
     for h in range(heads):
-        wide[h] = jnp.full((8, E), rates[h], F32)
-        scale[h] = power(rates[h], BLOCK - 1.0 - inner)
-    for b in range(count):
-        rows = pl.ds(b * BLOCK, BLOCK)
-        for copy in copies(b):
-            copy.wait()
-        for h in range(heads):
-            scaled = keys[rows, head_columns(h)].astype(F32) * scale[h]
+        rate = jnp.broadcast_to(rates[0:1, h : h + 1], (8, E))
+        wide[h] = rate
+        scale = power(rate[0:1], BLOCK - 1.0 - inner[...])
+        decay = power(rate[0:1], float(BLOCK))
+        total = None
+        for b in range(count):
+            rows = pl.ds(b * BLOCK, BLOCK)
+            scaled = keys[rows, head_columns(h)].astype(F32) * scale
             block = lax.dot_general(
                 scaled.astype(BF16),
                 values[rows, head_columns(h)],
                 (((0,), (0,)), ((), ())),
                 preferred_element_type=F32,
             )
-            if b > 0:
-                block = state[h] * power(wide[h, 0:1], float(BLOCK)) + block
-            state[h] = block
+            total = block if b == 0 else total * decay + block
+        state[h] = total
 
 
 def chip_kernel(length, half, wide, both, total):
@@ -208,12 +194,10 @@
         for h in range(out.shape[1] // E):
             part = mixed[rows, head_columns(h)] * column * gain[:, head_columns(h)]
             out[rows, head_columns(h)] = part.astype(BF16)
-        if t % 2 == 1:
-            pair = pl.ds((t - 1) * E, 2 * E)
-            pltpu.make_async_copy(out.at[pair], out_hbm.at[pair], sems.at[t // 2]).start()
-    for t in range(1, tiles, 2):
-        pair = pl.ds((t - 1) * E, 2 * E)
-        pltpu.make_async_copy(out.at[pair], out_hbm.at[pair], sems.at[t // 2]).wait()
+        pltpu.make_async_copy(out.at[rows], out_hbm.at[rows], sems.at[t]).start()
+    for t in range(tiles):
+        rows = pl.ds(t * E, E)
+        pltpu.make_async_copy(out.at[rows], out_hbm.at[rows], sems.at[t]).wait()
 
 
 def body(queries, key_rows, value_rows, decay_rates, out_gain):
@@ -225,27 +209,24 @@
     parts = lax.axis_size(HEAD)
     shape = jax.ShapeDtypeStruct
 
+    inner = call(
+        positions_kernel,
+        shape((BLOCK, E), F32),
+        [],
+        VMEM,
+        flops=DECAY_FLOPS,
+        moved=DECAY_MOVED,
+        name="positions",
+    )()
     state, wide = call(
         functools.partial(states_kernel, count, heads),
-        (
-            shape((heads, E, E), F32),
-            shape((heads, 8, E), F32),
-        ),
-        [HBM, HBM, HBM],
+        (shape((heads, E, E), F32), shape((heads, 8, E), F32)),
+        [VMEM] * 4,
         (VMEM, VMEM),
-        [
-            pltpu.VMEM((length, width), BF16),
-            pltpu.VMEM((length, width), BF16),
-            pltpu.VMEM((heads, BLOCK, E), F32),
-            pltpu.SMEM((heads,), F32),
-            pltpu.SemaphoreType.DMA((2, count)),
-            pltpu.SemaphoreType.DMA,
-        ],
-        room=STATES_ROOM,
         flops=2 * length * E * width,
         moved=4 * length * width,
         name="states",
-    )(decay_rates, key_rows, value_rows)
+    )(inner, decay_rates.reshape(1, heads), key_rows, value_rows)
     both = lax.all_gather(state, "c")
     total = call(
         functools.partial(chip_kernel, length, half),
@@ -313,7 +294,7 @@
         shape((length, width), BF16),
         [VMEM, VMEM, VMEM],
         HBM,
-        [pltpu.VMEM((length, width), BF16), pltpu.SemaphoreType.DMA((count,))],
+        [pltpu.VMEM((length, width), BF16), pltpu.SemaphoreType.DMA((length // E,))],
         moved=6 * length * width,
         name="norm",
     )(mixed, shared, out_gain.reshape(1, width))

time: 63.1 us -> 62.5 us (level)
  Pallas kernels: 7.62 us -> 6.11 us
  local copies, waits for them, and re-layouts: 2.26 us -> 3.12 us
    pallas_call x1, Pallas kernels: 2.23 us -> 0.69 us  [body(): call(functools.partial(states_kernel, count, heads), (shape((heads, E, E)...]
    unnamed x12 -> x16, local copies, waits for them, and re-layouts: 2.26 us -> 3.12 us
where the time goes in v5:
time: 62.5 us; the launch traced here: 62.2 us
  blocking collectives  44 us (70%)
  Pallas kernels  6.11 us (10%)
  waiting for transfers between devices  5.02 us (8%)
  starting transfers between devices  3.88 us (6%)
  local copies, waits for them, and re-layouts  3.12 us (5%)
    all_to_all x1, blocking collectives, body(): owned = lax.all_to_all(total.reshape(chips, -1, E), CHIPS, 0, 0, tiled=True)  16.7 us
    all_to_all x1, blocking collectives, body(): shared = lax.all_to_all(squares, HEAD, 0, 0, tiled=True)  13.6 us
    all_gather x1, blocking collectives, body(): both = lax.all_gather(state, 'c')  8.65 us
    all_gather x1, blocking collectives, body(): prefix = lax.all_gather(mine, 'c', tiled=True)  5.09 us
    all_to_all x1, waiting for transfers between devices, body(): mine = lax.all_to_all(prefixes, CHIPS, 0, 0, tiled=True).reshape(half, E, E)  5.02 us
    all_to_all x1, starting transfers between devices, body(): mine = lax.all_to_all(prefixes, CHIPS, 0, 0, tiled=True).reshape(half, E, E)  3.88 us
    unnamed x16, local copies, waits for them, and re-layouts  3.12 us
    pallas_call x1, Pallas kernels, body(): call(functools.partial(local_kernel, count, heads), shape((length, width)...  2.46 us
  transfers between devices with their start and end apart: 1, of which 1 were waited for; matrix products, arithmetic and copies ran while one was open for 0% of the time, Pallas kernels for 4%

profile of v5, /device:TPU:1, one launch (start us, length us, event | category | flops | bytes accessed | tf_op | source)
XLA Modules:
  0.0 62.2 jit_solution(2829647696970013793)
XLA Ops:
  0.0 0.0 copy-start.2
  0.0 0.0 copy-start
  0.0 0.0 copy-start.7
  0.0 1.2 %copy-done.2 = bf16[1024,512]{1,0:T(8,128)(2,1)S(1)} copy-done((bf16[1024,512]{1,0:T(8,128)(2,1)S(1)}, bf16[1024,512]{1,0:T(8,128)(2,1)}, u32[]{:S(2)}) %copy-start.2) | copy-done | bytes 1048600
  1.2 0.3 copy-done
  1.5 0.0 copy-done.7
  1.5 0.7 %states.1 = (f32[4,128,128]{2,1,0:T(8,128)S(1)}, f32[4,8,128]{2,1,0:T(8,128)S(1)}) custom-call(f32[256,128]{1,0:T(8,128)S(1)} %positions.1.inner, f32[1,4]{1,0:T(1,128)S(1)} %bitcast.10, bf16[1024,512]{1,0:T(8,128)(2,1)S(1)} %copy-done, bf16[1024,512]{1,0:T(8,128)(2,1)S(1)} %copy-done.2), custom_call_target="tpu_custom_call" | custom-call | flops 134217728 | bytes 2097152 | tf_op jit(solution)/shard_map/states/pallas_call | solution.py:221
  2.2 8.6 %all-gather = f32[8,128,128]{2,1,0:T(8,128)S(1)} all-gather(f32[4,128,128]{2,1,0:T(8,128)S(1)} %get-tuple-element.18), channel_id=2, replica_groups=mesh['z'=8,'x'=4,'c'=2,'head'=8] {'c'}, dimensions={0}, use_global_device_ids=true | all-gather | bytes 786432 | tf_op jit(solution)/shard_map/all_gather | solution.py:230
  10.9 16.7 %all_to_all.15.totals = f32[32,8,128]{2,1,0:T(8,128)S(1)} all-to-all(f32[32,8,128]{2,1,0:T(8,128)S(1)} %bitcast.7), channel_id=1, replica_groups=mesh['z'=8,'x'=4,'c'=2,'head'=8] {'z','x'}, dimensions={0} | all-to-all | bytes 262144 | tf_op jit(solution)/shard_map/all_to_all | solution.py:238
  27.6 0.7 %scan.1 = f32[32,8,128]{2,1,0:T(8,128)} custom-call(f32[4,8,128]{2,1,0:T(8,128)S(1)} %get-tuple-element.13.wide, f32[32,8,128]{2,1,0:T(8,128)S(1)} %all_to_all.15.totals), custom_call_target="tpu_custom_call" | custom-call | tf_op jit(solution)/shard_map/scan/pallas_call | solution.py:239
  28.3 3.9 %all-to-all-start.1 = ((f32[32,8,128]{2,1,0:T(8,128)}), f32[32,8,128]{2,1,0:T(8,128)S(1)}, u32[]{:S(2)}, u32[]{:S(2)}) async-start(f32[32,8,128]{2,1,0:T(8,128)} %scan.1), calls=%async_computation.1 | async-start | bytes 262144 | tf_op jit(solution)/shard_map/all_to_all | solution.py:246
  32.2 0.0 copy-start.1
  32.2 0.0 copy-start.3
  32.2 0.0 copy-start.4
  32.3 0.2 decays.1
  32.5 0.9 %copy-done.1 = bf16[1024,512]{1,0:T(8,128)(2,1)S(1)} copy-done((bf16[1024,512]{1,0:T(8,128)(2,1)S(1)}, bf16[1024,512]{1,0:T(8,128)(2,1)}, u32[]{:S(2)}) %copy-start.1) | copy-done | bytes 1048600
  33.4 0.3 copy-done.3
  33.8 0.3 copy-done.4
  34.1 2.5 %local.1 = f32[1024,512]{1,0:T(8,128)S(1)} custom-call(f32[4,8,128]{2,1,0:T(8,128)S(1)} %get-tuple-element.13.wide, f32[4,128,128]{2,1,0:T(8,128)S(1)} %get-tuple-element.15.within, f32[4,128,128]{2,1,0:T(8,128)S(1)} %get-tuple-element.16.across, f32[4,256,128]{2,1,0:T(8,128)S(1)} %get-tuple-element.14.scale, ...), custom_call_target="tpu_custom_call" | custom-call | flops 1073741824 | bytes 5242880 | tf_op jit(solution)/shard_map/local/pallas_call | solution.py:271
  36.5 5.0 %all-to-all-done.1 = f32[32,8,128]{2,1,0:T(8,128)S(1)} async-done(((f32[32,8,128]{2,1,0:T(8,128)}), f32[32,8,128]{2,1,0:T(8,128)S(1)}, u32[]{:S(2)}, u32[]{:S(2)}) %all-to-all-start.1) | async-done | bytes 131104 | tf_op jit(solution)/shard_map/all_to_all | solution.py:246
  41.6 0.0 copy-start.5
  41.6 5.1 %all_gather.11.prefix = f32[4,128,128]{2,1,0:T(8,128)S(1)} all-gather(f32[2,128,128]{2,1,0:T(8,128)S(1)} %relay.1), channel_id=1, replica_groups=mesh['z'=8,'x'=4,'c'=2,'head'=8] {'c'}, dimensions={0}, use_global_device_ids=true | all-gather | bytes 393216 | tf_op jit(solution)/shard_map/all_gather | solution.py:256
  46.7 0.0 copy-done.5
  46.7 0.0 copy-start.6
  46.7 0.8 %mix.1 = (f32[1024,512]{1,0:T(8,128)S(1)}, f32[8,8,128]{2,1,0:T(8,128)S(1)}) custom-call(f32[4,8,128]{2,1,0:T(8,128)S(1)} %get-tuple-element.13.wide, f32[4,256,128]{2,1,0:T(8,128)S(1)} %get-tuple-element.14.scale, bf16[1024,512]{1,0:T(8,128)(2,1)S(1)} %copy-done.5, f32[1024,512]{1,0:T(8,128)S(1)} %local.1, f32[4,128,128]{2,1,0:T(8,128)S(1)} %all_gather.11.prefix), custom_call_target="tpu_custom_call" | custom-call | flops 268435456 | bytes 5242880 | tf_op jit(solution)/shard_map/mix/pallas_call | solution.py:282
  47.5 13.6 %all_to_all.16.squares = f32[8,8,128]{2,1,0:T(8,128)S(1)} all-to-all(f32[8,8,128]{2,1,0:T(8,128)S(1)} %get-tuple-element.20), channel_id=1, replica_groups=mesh['z'=8,'x'=4,'c'=2,'head'=8] {'head'}, dimensions={0} | all-to-all | bytes 65536 | tf_op jit(solution)/shard_map/all_to_all | solution.py:291
  61.0 0.0 copy-done.6
  61.0 1.2 %norm.1 = bf16[1024,512]{1,0:T(8,128)(2,1)} custom-call(f32[1024,512]{1,0:T(8,128)S(1)} %get-tuple-element.19.mixed, f32[8,8,128]{2,1,0:T(8,128)S(1)} %all_to_all.16.squares, f32[1,512]{1,0:T(1,128)S(1)} %bitcast.9), custom_call_target="tpu_custom_call" | custom-call | bytes 3145728 | tf_op jit(solution)/shard_map/norm/pallas_call | solution.py:292
  (3 shorter events, 0.0 us)
Async XLA Ops:
  0.0 1.2 %copy-start.2 = (bf16[1024,512]{1,0:T(8,128)(2,1)S(1)}, bf16[1024,512]{1,0:T(8,128)(2,1)}, u32[]{:S(2)}) copy-start(bf16[1024,512]{1,0:T(8,128)(2,1)} %values.3) | copy-start | bytes 3145732
  0.0 1.5 %copy-start = (bf16[1024,512]{1,0:T(8,128)(2,1)S(1)}, bf16[1024,512]{1,0:T(8,128)(2,1)}, u32[]{:S(2)}) copy-start(bf16[1024,512]{1,0:T(8,128)(2,1)} %keys.3) | copy-start | bytes 3145732
  0.0 1.5 %copy-start.7 = (f32[4]{0:T(128)S(1)}, f32[4]{0:T(128)}, u32[]{:S(2)}) copy-start(f32[4]{0:T(128)} %param.8) | copy-start | bytes 52
  28.3 13.2 %all-to-all-start.1 = ((f32[32,8,128]{2,1,0:T(8,128)}), f32[32,8,128]{2,1,0:T(8,128)S(1)}, u32[]{:S(2)}, u32[]{:S(2)}) async-start(f32[32,8,128]{2,1,0:T(8,128)} %scan.1), calls=%async_computation.1 | async-start | bytes 262144 | tf_op jit(solution)/shard_map/all_to_all | solution.py:246
  32.2 1.2 %copy-start.1 = (bf16[1024,512]{1,0:T(8,128)(2,1)S(1)}, bf16[1024,512]{1,0:T(8,128)(2,1)}, u32[]{:S(2)}) copy-start(bf16[1024,512]{1,0:T(8,128)(2,1)} %keys.3) | copy-start | bytes 3145732
  32.2 1.5 %copy-start.3 = (bf16[1024,512]{1,0:T(8,128)(2,1)S(1)}, bf16[1024,512]{1,0:T(8,128)(2,1)}, u32[]{:S(2)}) copy-start(bf16[1024,512]{1,0:T(8,128)(2,1)} %values.3) | copy-start | bytes 3145732
  32.2 1.8 %copy-start.4 = (bf16[1024,512]{1,0:T(8,128)(2,1)S(1)}, bf16[1024,512]{1,0:T(8,128)(2,1)}, u32[]{:S(2)}) copy-start(bf16[1024,512]{1,0:T(8,128)(2,1)} %queries.3) | copy-start | bytes 3145732
  41.6 5.1 %copy-start.5 = (bf16[1024,512]{1,0:T(8,128)(2,1)S(1)}, bf16[1024,512]{1,0:T(8,128)(2,1)}, u32[]{:S(2)}) copy-start(bf16[1024,512]{1,0:T(8,128)(2,1)} %queries.3) | copy-start | bytes 3145732
  46.7 14.4 %copy-start.6 = (f32[512]{0:T(512)S(1)}, f32[512]{0:T(512)}, u32[]{:S(2)}) copy-start(f32[512]{0:T(512)} %param.9) | copy-start | bytes 6148

commit v6 on v5

--- a/solution.py
+++ b/solution.py
@@ -49,24 +49,22 @@
 
 
 def positions_kernel(inner):
-    inner[...] = lax.broadcasted_iota(jnp.int32, inner.shape, 0).astype(F32)
+    inner[...] = lax.broadcasted_iota(jnp.int32, inner.shape, 1).astype(F32)
 
 
 def states_kernel(count, heads, inner, rates, keys, values, state, wide):
     for h in range(heads):
         rate = jnp.broadcast_to(rates[0:1, h : h + 1], (8, E))
         wide[h] = rate
-        scale = power(rate[0:1], BLOCK - 1.0 - inner[...])
+        long_rate = jnp.concatenate([rate[0:1]] * (BLOCK // E), axis=1)
+        scale = power(long_rate, BLOCK - 1.0 - inner[0:1])
         decay = power(rate[0:1], float(BLOCK))
         total = None
         for b in range(count):
             rows = pl.ds(b * BLOCK, BLOCK)
-            scaled = keys[rows, head_columns(h)].astype(F32) * scale
-            block = lax.dot_general(
-                scaled.astype(BF16),
-                values[rows, head_columns(h)],
-                (((0,), (0,)), ((), ())),
-                preferred_element_type=F32,
+            scaled = keys[rows, head_columns(h)].T.astype(F32) * scale
+            block = jnp.dot(
+                scaled.astype(BF16), values[rows, head_columns(h)], preferred_element_type=F32
             )
             total = block if b == 0 else total * decay + block
         state[h] = total
@@ -156,7 +154,7 @@
     prefix[...] = mine[...]
 
 
-def mix_kernel(count, heads, wide, scale, queries, local, prefix, mixed, squares):
+def mix_kernel(count, heads, wide, scale, queries, local, prefix, gain, mixed, squares):
     length = float(count * BLOCK)
     second = lax.axis_index("c") == 1
     entering = []
@@ -175,14 +173,14 @@
             if block > 0:
                 factor = factor * power(wide[h, 0:1], float(block * BLOCK))
             out = local[rows, head_columns(h)] + out * factor
-            mixed[rows, head_columns(h)] = out
+            mixed[rows, head_columns(h)] = out * gain[:, head_columns(h)]
             total = total + out * out
         for r in range(ROWS // E):
             sums = jnp.sum(total[r * E : (r + 1) * E].T, axis=0, keepdims=True)
             squares[:, t * (ROWS // E) + r, :] = jnp.broadcast_to(sums, (squares.shape[0], E))
 
 
-def norm_kernel(count, mixed, squares, gain, out_hbm, out, sems):
+def norm_kernel(mixed, squares, out_hbm, out, sems):
     sums = squares[0]
     for i in range(1, squares.shape[0]):
         sums = sums + squares[i]
@@ -192,7 +190,7 @@
         rows = pl.ds(t * E, E)
         column = jnp.broadcast_to(inverse[t : t + 1, :], (E, E)).T
         for h in range(out.shape[1] // E):
-            part = mixed[rows, head_columns(h)] * column * gain[:, head_columns(h)]
+            part = mixed[rows, head_columns(h)] * column
             out[rows, head_columns(h)] = part.astype(BF16)
         pltpu.make_async_copy(out.at[rows], out_hbm.at[rows], sems.at[t]).start()
     for t in range(tiles):
@@ -211,7 +209,7 @@
 
     inner = call(
         positions_kernel,
-        shape((BLOCK, E), F32),
+        shape((8, BLOCK), F32),
         [],
         VMEM,
         flops=DECAY_FLOPS,
@@ -282,22 +280,22 @@
     mixed, squares = call(
         functools.partial(mix_kernel, count, heads),
         (shape((length, width), F32), shape((parts, length // E, E), F32)),
-        [VMEM] * 5,
+        [VMEM] * 6,
         (VMEM, VMEM),
         flops=4 * length * E * width,
         moved=10 * length * width,
         name="mix",
-    )(wide, decays[2], queries, local, prefix)
+    )(wide, decays[2], queries, local, prefix, out_gain.reshape(1, width))
     shared = lax.all_to_all(squares, HEAD, 0, 0, tiled=True)
     return call(
-        functools.partial(norm_kernel, count),
+        norm_kernel,
         shape((length, width), BF16),
-        [VMEM, VMEM, VMEM],
+        [VMEM, VMEM],
         HBM,
         [pltpu.VMEM((length, width), BF16), pltpu.SemaphoreType.DMA((length // E,))],
         moved=6 * length * width,
         name="norm",
-    )(mixed, shared, out_gain.reshape(1, width))
+    )(mixed, shared)
 
 
 def solution(mesh):

time: 62.5 us -> 62.3 us (level)
  no operation moved by 1% of the time
where the time goes in v6:
time: 62.3 us; the launch traced here: 62 us
  blocking collectives  44 us (71%)
  Pallas kernels  5.95 us (10%)
  waiting for transfers between devices  5.02 us (8%)
  starting transfers between devices  3.88 us (6%)
  local copies, waits for them, and re-layouts  3.13 us (5%)
    all_to_all x1, blocking collectives, body(): owned = lax.all_to_all(total.reshape(chips, -1, E), CHIPS, 0, 0, tiled=True)  16.7 us
    all_to_all x1, blocking collectives, body(): shared = lax.all_to_all(squares, HEAD, 0, 0, tiled=True)  13.6 us
    all_gather x1, blocking collectives, body(): both = lax.all_gather(state, 'c')  8.65 us
    all_gather x1, blocking collectives, body(): prefix = lax.all_gather(mine, 'c', tiled=True)  5.09 us
    all_to_all x1, waiting for transfers between devices, body(): mine = lax.all_to_all(prefixes, CHIPS, 0, 0, tiled=True).reshape(half, E, E)  5.02 us
    all_to_all x1, starting transfers between devices, body(): mine = lax.all_to_all(prefixes, CHIPS, 0, 0, tiled=True).reshape(half, E, E)  3.88 us
    unnamed x16, local copies, waits for them, and re-layouts  3.13 us
    pallas_call x1, Pallas kernels, body(): call(functools.partial(local_kernel, count, heads), shape((length, width)...  2.46 us
  transfers between devices with their start and end apart: 1, of which 1 were waited for; matrix products, arithmetic and copies ran while one was open for 0% of the time, Pallas kernels for 4%

profile of v6, /device:TPU:1, one launch (start us, length us, event | category | flops | bytes accessed | tf_op | source)
XLA Modules:
  0.0 62.0 jit_solution(7572986907149027106)
XLA Ops:
  0.0 0.0 copy-start.4
  0.0 0.0 copy-start.2
  0.0 0.0 copy-start.7
  0.0 1.2 %copy-done.4 = bf16[1024,512]{1,0:T(8,128)(2,1)S(1)} copy-done((bf16[1024,512]{1,0:T(8,128)(2,1)S(1)}, bf16[1024,512]{1,0:T(8,128)(2,1)}, u32[]{:S(2)}) %copy-start.4) | copy-done | bytes 1048600
  1.2 0.3 copy-done.2
  1.5 0.0 copy-done.7
  1.5 0.5 states.1
  2.1 8.6 %all-gather = f32[8,128,128]{2,1,0:T(8,128)S(1)} all-gather(f32[4,128,128]{2,1,0:T(8,128)S(1)} %get-tuple-element.18), channel_id=2, replica_groups=mesh['z'=8,'x'=4,'c'=2,'head'=8] {'c'}, dimensions={0}, use_global_device_ids=true | all-gather | bytes 786432 | tf_op jit(solution)/shard_map/all_gather | solution.py:228
  10.8 16.7 %all_to_all.15.totals = f32[32,8,128]{2,1,0:T(8,128)S(1)} all-to-all(f32[32,8,128]{2,1,0:T(8,128)S(1)} %bitcast.7), channel_id=1, replica_groups=mesh['z'=8,'x'=4,'c'=2,'head'=8] {'z','x'}, dimensions={0} | all-to-all | bytes 262144 | tf_op jit(solution)/shard_map/all_to_all | solution.py:236
  27.4 0.7 %scan.1 = f32[32,8,128]{2,1,0:T(8,128)} custom-call(f32[4,8,128]{2,1,0:T(8,128)S(1)} %get-tuple-element.13.wide, f32[32,8,128]{2,1,0:T(8,128)S(1)} %all_to_all.15.totals), custom_call_target="tpu_custom_call" | custom-call | tf_op jit(solution)/shard_map/scan/pallas_call | solution.py:237
  28.2 3.9 %all-to-all-start.1 = ((f32[32,8,128]{2,1,0:T(8,128)}), f32[32,8,128]{2,1,0:T(8,128)S(1)}, u32[]{:S(2)}, u32[]{:S(2)}) async-start(f32[32,8,128]{2,1,0:T(8,128)} %scan.1), calls=%async_computation.1 | async-start | bytes 262144 | tf_op jit(solution)/shard_map/all_to_all | solution.py:244
  32.1 0.0 copy-start
  32.1 0.0 copy-start.3
  32.1 0.0 copy-start.5
  32.1 0.2 decays.1
  32.4 0.9 %copy-done = bf16[1024,512]{1,0:T(8,128)(2,1)S(1)} copy-done((bf16[1024,512]{1,0:T(8,128)(2,1)S(1)}, bf16[1024,512]{1,0:T(8,128)(2,1)}, u32[]{:S(2)}) %copy-start) | copy-done | bytes 1048600
  33.3 0.3 copy-done.3
  33.6 0.3 copy-done.5
  33.9 2.5 %local.1 = f32[1024,512]{1,0:T(8,128)S(1)} custom-call(f32[4,8,128]{2,1,0:T(8,128)S(1)} %get-tuple-element.13.wide, f32[4,128,128]{2,1,0:T(8,128)S(1)} %get-tuple-element.15.within, f32[4,128,128]{2,1,0:T(8,128)S(1)} %get-tuple-element.16.across, f32[4,256,128]{2,1,0:T(8,128)S(1)} %get-tuple-element.14.scale, ...), custom_call_target="tpu_custom_call" | custom-call | flops 1073741824 | bytes 5242880 | tf_op jit(solution)/shard_map/local/pallas_call | solution.py:269
  36.4 5.0 %all-to-all-done.1 = f32[32,8,128]{2,1,0:T(8,128)S(1)} async-done(((f32[32,8,128]{2,1,0:T(8,128)}), f32[32,8,128]{2,1,0:T(8,128)S(1)}, u32[]{:S(2)}, u32[]{:S(2)}) %all-to-all-start.1) | async-done | bytes 131104 | tf_op jit(solution)/shard_map/all_to_all | solution.py:244
  41.4 0.0 copy-start.1
  41.4 0.0 copy-start.6
  41.4 5.1 %all_gather.11.prefix = f32[4,128,128]{2,1,0:T(8,128)S(1)} all-gather(f32[2,128,128]{2,1,0:T(8,128)S(1)} %relay.1), channel_id=1, replica_groups=mesh['z'=8,'x'=4,'c'=2,'head'=8] {'c'}, dimensions={0}, use_global_device_ids=true | all-gather | bytes 393216 | tf_op jit(solution)/shard_map/all_gather | solution.py:254
  46.5 0.0 copy-done.1
  46.5 0.0 copy-done.6
  46.5 0.8 %mix.1 = (f32[1024,512]{1,0:T(8,128)S(1)}, f32[8,8,128]{2,1,0:T(8,128)S(1)}) custom-call(f32[4,8,128]{2,1,0:T(8,128)S(1)} %get-tuple-element.13.wide, f32[4,256,128]{2,1,0:T(8,128)S(1)} %get-tuple-element.14.scale, bf16[1024,512]{1,0:T(8,128)(2,1)S(1)} %copy-done.1, f32[1024,512]{1,0:T(8,128)S(1)} %local.1, f32[4,128,128]{2,1,0:T(8,128)S(1)} %all_gather.11.prefix, ...), custom_call_target="tpu_custom_call" | custom-call | flops 268435456 | bytes 5242880 | tf_op jit(solution)/shard_map/mix/pallas_call | solution.py:280
  47.3 13.6 %all_to_all.16.squares = f32[8,8,128]{2,1,0:T(8,128)S(1)} all-to-all(f32[8,8,128]{2,1,0:T(8,128)S(1)} %get-tuple-element.20), channel_id=1, replica_groups=mesh['z'=8,'x'=4,'c'=2,'head'=8] {'head'}, dimensions={0} | all-to-all | bytes 65536 | tf_op jit(solution)/shard_map/all_to_all | solution.py:289
  60.9 1.1 %norm.1 = bf16[1024,512]{1,0:T(8,128)(2,1)} custom-call(f32[1024,512]{1,0:T(8,128)S(1)} %get-tuple-element.19.mixed, f32[8,8,128]{2,1,0:T(8,128)S(1)} %all_to_all.16.squares), custom_call_target="tpu_custom_call" | custom-call | bytes 3145728 | tf_op jit(solution)/shard_map/norm/pallas_call | solution.py:290
  (3 shorter events, 0.0 us)
Async XLA Ops:
  0.0 1.2 %copy-start.4 = (bf16[1024,512]{1,0:T(8,128)(2,1)S(1)}, bf16[1024,512]{1,0:T(8,128)(2,1)}, u32[]{:S(2)}) copy-start(bf16[1024,512]{1,0:T(8,128)(2,1)} %values.3) | copy-start | bytes 3145732
  0.0 1.5 %copy-start.2 = (bf16[1024,512]{1,0:T(8,128)(2,1)S(1)}, bf16[1024,512]{1,0:T(8,128)(2,1)}, u32[]{:S(2)}) copy-start(bf16[1024,512]{1,0:T(8,128)(2,1)} %keys.3) | copy-start | bytes 3145732
  0.0 1.5 %copy-start.7 = (f32[4]{0:T(128)S(1)}, f32[4]{0:T(128)}, u32[]{:S(2)}) copy-start(f32[4]{0:T(128)} %param.8) | copy-start | bytes 52
  28.2 13.2 %all-to-all-start.1 = ((f32[32,8,128]{2,1,0:T(8,128)}), f32[32,8,128]{2,1,0:T(8,128)S(1)}, u32[]{:S(2)}, u32[]{:S(2)}) async-start(f32[32,8,128]{2,1,0:T(8,128)} %scan.1), calls=%async_computation.1 | async-start | bytes 262144 | tf_op jit(solution)/shard_map/all_to_all | solution.py:244
  32.1 1.2 %copy-start = (bf16[1024,512]{1,0:T(8,128)(2,1)S(1)}, bf16[1024,512]{1,0:T(8,128)(2,1)}, u32[]{:S(2)}) copy-start(bf16[1024,512]{1,0:T(8,128)(2,1)} %queries.3) | copy-start | bytes 3145732
  32.1 1.5 %copy-start.3 = (bf16[1024,512]{1,0:T(8,128)(2,1)S(1)}, bf16[1024,512]{1,0:T(8,128)(2,1)}, u32[]{:S(2)}) copy-start(bf16[1024,512]{1,0:T(8,128)(2,1)} %keys.3) | copy-start | bytes 3145732
  32.1 1.8 %copy-start.5 = (bf16[1024,512]{1,0:T(8,128)(2,1)S(1)}, bf16[1024,512]{1,0:T(8,128)(2,1)}, u32[]{:S(2)}) copy-start(bf16[1024,512]{1,0:T(8,128)(2,1)} %values.3) | copy-start | bytes 3145732
  41.4 5.1 %copy-start.1 = (bf16[1024,512]{1,0:T(8,128)(2,1)S(1)}, bf16[1024,512]{1,0:T(8,128)(2,1)}, u32[]{:S(2)}) copy-start(bf16[1024,512]{1,0:T(8,128)(2,1)} %queries.3) | copy-start | bytes 3145732
  41.4 5.1 %copy-start.6 = (f32[512]{0:T(512)S(1)}, f32[512]{0:T(512)}, u32[]{:S(2)}) copy-start(f32[512]{0:T(512)} %param.9) | copy-start | bytes 6148

commit v7 on v6

--- a/solution.py
+++ b/solution.py
@@ -52,7 +52,7 @@
     inner[...] = lax.broadcasted_iota(jnp.int32, inner.shape, 1).astype(F32)
 
 
-def states_kernel(count, heads, inner, rates, keys, values, state, wide):
+def states_kernel(count, heads, inner, rates, keys, values, state, given, wide):
     for h in range(heads):
         rate = jnp.broadcast_to(rates[0:1, h : h + 1], (8, E))
         wide[h] = rate
@@ -68,13 +68,19 @@
             )
             total = block if b == 0 else total * decay + block
         state[h] = total
-
-
-def chip_kernel(length, half, wide, both, total):
-    first = lax.axis_index("c") * half
+    half = heads // 2
+    first_core = lax.axis_index("c") == 0
     for i in range(half):
-        decay = power(wide[first + i, 0:1], float(length))
-        total[i] = both[0, first + i] * decay + both[1, first + i]
+        given[i] = jnp.where(first_core, state[half + i], state[i])
+
+
+def chip_kernel(length, half, wide, state, both, total, first):
+    core = lax.axis_index("c")
+    for i in range(half):
+        decay = power(wide[core * half + i, 0:1], float(length))
+        before = jnp.where(core == 0, state[i], both[0, i])
+        first[i] = before
+        total[i] = before * decay + jnp.where(core == 0, both[1, i], state[half + i])
 
 
 def scan_kernel(length, half, chips, wide, totals, prefixes):
@@ -113,11 +119,8 @@
 
 
 def local_kernel(
-    count, heads, wide, within, across, scale, key_scale, both, queries, keys, values, local, held
+    count, heads, wide, within, across, scale, key_scale, queries, keys, values, local, held
 ):
-    second = lax.axis_index("c") == 1
-    for h in range(heads):
-        held[h] = jnp.where(second, both[0, h], 0.0)
     top, bottom = slice(0, E), slice(E, BLOCK)
     for b in range(count):
         rows = pl.ds(b * BLOCK, BLOCK)
@@ -139,27 +142,36 @@
                 axis=0,
             )
             out = jnp.dot(weights, value, preferred_element_type=F32)
-            doubled = jnp.concatenate([query, query], axis=1)
-            carried = jnp.dot(doubled, two_halves(held[h]), preferred_element_type=F32)
-            local[rows, head_columns(h)] = out + carried * scale[h]
+            if b > 0:
+                doubled = jnp.concatenate([query, query], axis=1)
+                carried = jnp.dot(doubled, two_halves(held[h]), preferred_element_type=F32)
+                out = out + carried * scale[h]
+            local[rows, head_columns(h)] = out
             if b < count - 1:
                 scaled = (key.astype(F32) * key_scale[h]).astype(BF16)
                 block = lax.dot_general(
                     scaled, value, (((0,), (0,)), ((), ())), preferred_element_type=F32
                 )
-                held[h] = held[h] * power(wide[h, 0:1], float(BLOCK)) + block
-
-
-def relay_kernel(mine, prefix):
-    prefix[...] = mine[...]
-
-
-def mix_kernel(count, heads, wide, scale, queries, local, prefix, gain, mixed, squares):
+                held[h] = held[h] * power(wide[h, 0:1], float(BLOCK)) + block if b > 0 else block
+
+
+def relay_kernel(length, half, wide, mine, first, given):
+    core = lax.axis_index("c")
+    for i in range(half):
+        decay = power(wide[i, 0:1], float(length))
+        given[i] = jnp.where(core == 0, mine[i] * decay + first[i], mine[i])
+
+
+def mix_kernel(count, heads, wide, scale, queries, local, mine, first, prefix, gain, mixed, squares):
     length = float(count * BLOCK)
     second = lax.axis_index("c") == 1
+    half = heads // 2
     entering = []
-    for h in range(heads):
-        entering.append(two_halves(prefix[h] * jnp.where(second, power(wide[h, 0:1], length), 1.0)))
+    for h in range(half):
+        entering.append(two_halves(jnp.where(second, prefix[h], mine[h])))
+    for h in range(half, heads):
+        decayed = mine[h - half] * power(wide[h, 0:1], length) + first[h - half]
+        entering.append(two_halves(jnp.where(second, decayed, prefix[h])))
     for t in range(count * BLOCK // ROWS):
         rows = pl.ds(t * ROWS, ROWS)
         inner = t * ROWS % BLOCK
@@ -216,23 +228,23 @@
         moved=DECAY_MOVED,
         name="positions",
     )()
-    state, wide = call(
+    state, given, wide = call(
         functools.partial(states_kernel, count, heads),
-        (shape((heads, E, E), F32), shape((heads, 8, E), F32)),
+        (shape((heads, E, E), F32), shape((half, E, E), F32), shape((heads, 8, E), F32)),
         [VMEM] * 4,
-        (VMEM, VMEM),
+        (VMEM,) * 3,
         flops=2 * length * E * width,
         moved=4 * length * width,
         name="states",
     )(inner, decay_rates.reshape(1, heads), key_rows, value_rows)
-    both = lax.all_gather(state, "c")
-    total = call(
+    both = lax.all_gather(given, "c")
+    total, first = call(
         functools.partial(chip_kernel, length, half),
-        shape((half, E, E), F32),
-        [VMEM, VMEM],
-        VMEM,
+        (shape((half, E, E), F32), shape((half, E, E), F32)),
+        [VMEM] * 3,
+        (VMEM, VMEM),
         name="chip",
-    )(wide, both)
+    )(wide, state, both)
     owned = lax.all_to_all(total.reshape(chips, -1, E), CHIPS, 0, 0, tiled=True)
     prefixes = call(
         functools.partial(scan_kernel, length, half, chips),
@@ -242,16 +254,16 @@
         name="scan",
     )(wide, owned)
     mine = lax.all_to_all(prefixes, CHIPS, 0, 0, tiled=True).reshape(half, E, E)
-    mine = call(
-        relay_kernel,
+    given = call(
+        functools.partial(relay_kernel, length, half),
         shape(mine.shape, F32),
-        [VMEM],
+        [VMEM] * 3,
         VMEM,
         flops=DECAY_FLOPS,
         moved=DECAY_MOVED,
         name="relay",
-    )(mine)
-    prefix = lax.all_gather(mine, "c", tiled=True)
+    )(wide, mine, first)
+    prefix = lax.all_gather(given, "c", tiled=True)
     decays = call(
         functools.partial(decay_kernel, heads),
         (
@@ -269,23 +281,23 @@
     local = call(
         functools.partial(local_kernel, count, heads),
         shape((length, width), F32),
-        [VMEM] * 9,
+        [VMEM] * 8,
         VMEM,
         [pltpu.VMEM((heads, E, E), F32)],
         room=LOCAL_ROOM,
         flops=8 * length * BLOCK * width,
         moved=10 * length * width,
         name="local",
-    )(wide, *decays, both, queries, key_rows, value_rows)
+    )(wide, *decays, queries, key_rows, value_rows)
     mixed, squares = call(
         functools.partial(mix_kernel, count, heads),
         (shape((length, width), F32), shape((parts, length // E, E), F32)),
-        [VMEM] * 6,
+        [VMEM] * 8,
         (VMEM, VMEM),
         flops=4 * length * E * width,
         moved=10 * length * width,
         name="mix",
-    )(wide, decays[2], queries, local, prefix, out_gain.reshape(1, width))
+    )(wide, decays[2], queries, local, mine, first, prefix, out_gain.reshape(1, width))
     shared = lax.all_to_all(squares, HEAD, 0, 0, tiled=True)
     return call(
         norm_kernel,

time: 62.3 us -> 62.2 us (level)
    unnamed x16 -> x18, local copies, waits for them, and re-layouts: 3.13 us -> 3.61 us
  transfers between devices with their start and end apart: 1 -> 1, of which waited for: 1 -> 1; matrix products, arithmetic and copies ran while one was open for 0% -> 0% of each run, Pallas kernels for 4% -> 5%
where the time goes in v7:
time: 62.2 us; the launch traced here: 61.8 us
  blocking collectives  43.7 us (70%)
  Pallas kernels  6.1 us (10%)
  waiting for transfers between devices  4.43 us (7%)
  starting transfers between devices  3.89 us (6%)
  local copies, waits for them, and re-layouts  3.61 us (6%)
    all_to_all x1, blocking collectives, body(): owned = lax.all_to_all(total.reshape(chips, -1, E), CHIPS, 0, 0, tiled=True)  16.7 us
    all_to_all x1, blocking collectives, body(): shared = lax.all_to_all(squares, HEAD, 0, 0, tiled=True)  13.6 us
    all_gather x1, blocking collectives, body(): both = lax.all_gather(given, 'c')  8.47 us
    all_gather x1, blocking collectives, body(): prefix = lax.all_gather(given, 'c', tiled=True)  5.02 us
    all_to_all x1, waiting for transfers between devices, body(): mine = lax.all_to_all(prefixes, CHIPS, 0, 0, tiled=True).reshape(half, E, E)  4.43 us
    all_to_all x1, starting transfers between devices, body(): mine = lax.all_to_all(prefixes, CHIPS, 0, 0, tiled=True).reshape(half, E, E)  3.89 us
    unnamed x18, local copies, waits for them, and re-layouts  3.61 us
    pallas_call x1, Pallas kernels, body(): call(functools.partial(local_kernel, count, heads), shape((length, width)...  2.57 us
  transfers between devices with their start and end apart: 1, of which 1 were waited for; matrix products, arithmetic and copies ran while one was open for 0% of the time, Pallas kernels for 5%

profile of v7, /device:TPU:1, one launch (start us, length us, event | category | flops | bytes accessed | tf_op | source)
XLA Modules:
  0.0 61.8 jit_solution(16363506579982504658)
XLA Ops:
  0.0 0.0 copy-start.1
  0.0 0.0 copy-start
  0.0 0.0 copy-start.8
  0.0 1.2 %copy-done.1 = bf16[1024,512]{1,0:T(8,128)(2,1)S(1)} copy-done((bf16[1024,512]{1,0:T(8,128)(2,1)S(1)}, bf16[1024,512]{1,0:T(8,128)(2,1)}, u32[]{:S(2)}) %copy-start.1) | copy-done | bytes 1048600
  1.2 0.3 copy-done
  1.5 0.0 copy-done.8
  1.5 0.5 states.1
  2.1 8.5 %all-gather = f32[4,128,128]{2,1,0:T(8,128)S(1)} all-gather(f32[2,128,128]{2,1,0:T(8,128)S(1)} %get-tuple-element.22), channel_id=2, replica_groups=mesh['z'=8,'x'=4,'c'=2,'head'=8] {'c'}, dimensions={0}, use_global_device_ids=true | all-gather | bytes 393216 | tf_op jit(solution)/shard_map/all_gather | solution.py:240
  10.6 16.7 %all_to_all.15.totals = f32[32,8,128]{2,1,0:T(8,128)S(1)} all-to-all(f32[32,8,128]{2,1,0:T(8,128)S(1)} %bitcast.8), channel_id=1, replica_groups=mesh['z'=8,'x'=4,'c'=2,'head'=8] {'z','x'}, dimensions={0} | all-to-all | bytes 262144 | tf_op jit(solution)/shard_map/all_to_all | solution.py:248
  27.3 0.7 %scan.1 = f32[32,8,128]{2,1,0:T(8,128)} custom-call(f32[4,8,128]{2,1,0:T(8,128)S(1)} %get-tuple-element.16.wide, f32[32,8,128]{2,1,0:T(8,128)S(1)} %all_to_all.15.totals), custom_call_target="tpu_custom_call" | custom-call | tf_op jit(solution)/shard_map/scan/pallas_call | solution.py:249
  28.0 3.9 %all-to-all-start.1 = ((f32[32,8,128]{2,1,0:T(8,128)}), f32[32,8,128]{2,1,0:T(8,128)S(1)}, u32[]{:S(2)}, u32[]{:S(2)}) async-start(f32[32,8,128]{2,1,0:T(8,128)} %scan.1), calls=%async_computation.1 | async-start | bytes 262144 | tf_op jit(solution)/shard_map/all_to_all | solution.py:256
  31.9 0.0 copy-start.2
  31.9 0.0 copy-start.3
  31.9 0.2 decays.1
  32.2 1.0 %copy-done.2 = bf16[1024,512]{1,0:T(8,128)(2,1)S(1)} copy-done((bf16[1024,512]{1,0:T(8,128)(2,1)S(1)}, bf16[1024,512]{1,0:T(8,128)(2,1)}, u32[]{:S(2)}) %copy-start.2) | copy-done | bytes 1048600
  33.1 0.3 copy-done.3
  33.5 2.6 %local.1 = f32[1024,512]{1,0:T(8,128)S(1)} custom-call(f32[4,8,128]{2,1,0:T(8,128)S(1)} %get-tuple-element.16.wide, f32[4,128,128]{2,1,0:T(8,128)S(1)} %get-tuple-element.18.within, f32[4,128,128]{2,1,0:T(8,128)S(1)} %get-tuple-element.19.across, f32[4,256,128]{2,1,0:T(8,128)S(1)} %get-tuple-element.17.scale, ...), custom_call_target="tpu_custom_call" | custom-call | flops 1073741824 | bytes 5242880 | tf_op jit(solution)/shard_map/local/pallas_call | solution.py:281
  36.0 0.0 copy-start.5
  36.0 0.8 %copy-done.5 = f32[4,256,128]{2,1,0:T(8,128)} copy-done((f32[4,256,128]{2,1,0:T(8,128)}, f32[4,256,128]{2,1,0:T(8,128)S(1)}, u32[]{:S(2)}) %copy-start.5) | copy-done | bytes 524312
  36.8 4.4 %all-to-all-done.1 = f32[32,8,128]{2,1,0:T(8,128)S(1)} async-done(((f32[32,8,128]{2,1,0:T(8,128)}), f32[32,8,128]{2,1,0:T(8,128)S(1)}, u32[]{:S(2)}, u32[]{:S(2)}) %all-to-all-start.1) | async-done | bytes 131104 | tf_op jit(solution)/shard_map/all_to_all | solution.py:256
  41.3 0.0 copy-start.4
  41.3 0.0 copy-start.6
  41.3 0.0 copy-start.7
  41.3 5.0 %all_gather.11.prefix = f32[4,128,128]{2,1,0:T(8,128)S(1)} all-gather(f32[2,128,128]{2,1,0:T(8,128)S(1)} %relay.1), channel_id=1, replica_groups=mesh['z'=8,'x'=4,'c'=2,'head'=8] {'c'}, dimensions={0}, use_global_device_ids=true | all-gather | bytes 393216 | tf_op jit(solution)/shard_map/all_gather | solution.py:266
  46.3 0.0 copy-done.4
  46.3 0.0 copy-done.6
  46.3 0.0 copy-done.7
  46.3 0.8 %mix.1 = (f32[1024,512]{1,0:T(8,128)S(1)}, f32[8,8,128]{2,1,0:T(8,128)S(1)}) custom-call(f32[4,8,128]{2,1,0:T(8,128)S(1)} %get-tuple-element.16.wide, f32[4,256,128]{2,1,0:T(8,128)S(1)} %copy-done.6, bf16[1024,512]{1,0:T(8,128)(2,1)S(1)} %copy-done.4, f32[1024,512]{1,0:T(8,128)S(1)} %local.1, f32[2,128,128]{2,1,0:T(8,128)S(1)} %bitcast.7, ...), custom_call_target="tpu_custom_call" | custom-call | flops 268435456 | bytes 5242880 | tf_op jit(solution)/shard_map/mix/pallas_call | solution.py:292
  47.1 13.6 %all_to_all.16.squares = f32[8,8,128]{2,1,0:T(8,128)S(1)} all-to-all(f32[8,8,128]{2,1,0:T(8,128)S(1)} %get-tuple-element.26), channel_id=1, replica_groups=mesh['z'=8,'x'=4,'c'=2,'head'=8] {'head'}, dimensions={0} | all-to-all | bytes 65536 | tf_op jit(solution)/shard_map/all_to_all | solution.py:301
  60.7 1.1 %norm.1 = bf16[1024,512]{1,0:T(8,128)(2,1)} custom-call(f32[1024,512]{1,0:T(8,128)S(1)} %get-tuple-element.25.mixed, f32[8,8,128]{2,1,0:T(8,128)S(1)} %all_to_all.16.squares), custom_call_target="tpu_custom_call" | custom-call | bytes 3145728 | tf_op jit(solution)/shard_map/norm/pallas_call | solution.py:302
  (3 shorter events, 0.1 us)
Async XLA Ops:
  0.0 1.2 %copy-start.1 = (bf16[1024,512]{1,0:T(8,128)(2,1)S(1)}, bf16[1024,512]{1,0:T(8,128)(2,1)}, u32[]{:S(2)}) copy-start(bf16[1024,512]{1,0:T(8,128)(2,1)} %values.3) | copy-start | bytes 3145732
  0.0 1.5 %copy-start = (bf16[1024,512]{1,0:T(8,128)(2,1)S(1)}, bf16[1024,512]{1,0:T(8,128)(2,1)}, u32[]{:S(2)}) copy-start(bf16[1024,512]{1,0:T(8,128)(2,1)} %keys.3) | copy-start | bytes 3145732
  0.0 1.5 %copy-start.8 = (f32[4]{0:T(128)S(1)}, f32[4]{0:T(128)}, u32[]{:S(2)}) copy-start(f32[4]{0:T(128)} %param.8) | copy-start | bytes 52
  28.0 13.2 %all-to-all-start.1 = ((f32[32,8,128]{2,1,0:T(8,128)}), f32[32,8,128]{2,1,0:T(8,128)S(1)}, u32[]{:S(2)}, u32[]{:S(2)}) async-start(f32[32,8,128]{2,1,0:T(8,128)} %scan.1), calls=%async_computation.1 | async-start | bytes 262144 | tf_op jit(solution)/shard_map/all_to_all | solution.py:256
  31.9 1.2 %copy-start.2 = (bf16[1024,512]{1,0:T(8,128)(2,1)S(1)}, bf16[1024,512]{1,0:T(8,128)(2,1)}, u32[]{:S(2)}) copy-start(bf16[1024,512]{1,0:T(8,128)(2,1)} %values.3) | copy-start | bytes 3145732
  31.9 1.5 %copy-start.3 = (bf16[1024,512]{1,0:T(8,128)(2,1)S(1)}, bf16[1024,512]{1,0:T(8,128)(2,1)}, u32[]{:S(2)}) copy-start(bf16[1024,512]{1,0:T(8,128)(2,1)} %queries.3) | copy-start | bytes 3145732
  36.0 0.8 %copy-start.5 = (f32[4,256,128]{2,1,0:T(8,128)}, f32[4,256,128]{2,1,0:T(8,128)S(1)}, u32[]{:S(2)}) copy-start(f32[4,256,128]{2,1,0:T(8,128)S(1)} %get-tuple-element.17.scale) | copy-start | bytes 1572868
  41.3 5.1 %copy-start.4 = (bf16[1024,512]{1,0:T(8,128)(2,1)S(1)}, bf16[1024,512]{1,0:T(8,128)(2,1)}, u32[]{:S(2)}) copy-start(bf16[1024,512]{1,0:T(8,128)(2,1)} %queries.3) | copy-start | bytes 3145732
  41.3 5.1 %copy-start.6 = (f32[4,256,128]{2,1,0:T(8,128)S(1)}, f32[4,256,128]{2,1,0:T(8,128)}, u32[]{:S(2)}) copy-start(f32[4,256,128]{2,1,0:T(8,128)} %copy-done.5) | copy-start | bytes 1572868
  41.3 5.1 %copy-start.7 = (f32[512]{0:T(512)S(1)}, f32[512]{0:T(512)}, u32[]{:S(2)}) copy-start(f32[512]{0:T(512)} %param.9) | copy-start | bytes 6148

commit v8 on v7

--- a/solution.py
+++ b/solution.py
@@ -21,6 +21,7 @@
 VMEM_BYTES = 67043328
 LOCAL_ROOM = 40 << 20
 ROWS = 128
+PARTS = 4
 DECAY_FLOPS = 1 << 30
 DECAY_MOVED = 8 << 20
 VMEM = pl.BlockSpec(memory_space=pltpu.VMEM)
@@ -52,19 +53,28 @@
     inner[...] = lax.broadcasted_iota(jnp.int32, inner.shape, 1).astype(F32)
 
 
-def states_kernel(count, heads, inner, rates, keys, values, state, given, wide):
+def keys_kernel(count, heads, inner, rates, keys, scaled, wide):
     for h in range(heads):
         rate = jnp.broadcast_to(rates[0:1, h : h + 1], (8, E))
         wide[h] = rate
         long_rate = jnp.concatenate([rate[0:1]] * (BLOCK // E), axis=1)
         scale = power(long_rate, BLOCK - 1.0 - inner[0:1])
-        decay = power(rate[0:1], float(BLOCK))
+        for b in range(count):
+            rows = pl.ds(b * BLOCK, BLOCK)
+            turned = keys[rows, head_columns(h)].T.astype(F32) * scale
+            scaled[h, :, b * BLOCK : (b + 1) * BLOCK] = turned.astype(BF16)
+
+
+def states_kernel(count, heads, wide, scaled, values, state, given):
+    for h in range(heads):
+        decay = power(wide[h, 0:1], float(BLOCK))
         total = None
         for b in range(count):
             rows = pl.ds(b * BLOCK, BLOCK)
-            scaled = keys[rows, head_columns(h)].T.astype(F32) * scale
             block = jnp.dot(
-                scaled.astype(BF16), values[rows, head_columns(h)], preferred_element_type=F32
+                scaled[h, :, b * BLOCK : (b + 1) * BLOCK],
+                values[rows, head_columns(h)],
+                preferred_element_type=F32,
             )
             total = block if b == 0 else total * decay + block
         state[h] = total
@@ -83,14 +93,23 @@
         total[i] = before * decay + jnp.where(core == 0, both[1, i], state[half + i])
 
 
-def scan_kernel(length, half, chips, wide, totals, prefixes):
+def scan_kernel(length, half, chips, wide, totals, prefixes_hbm, prefixes, sems):
     piece = lax.axis_index("z") * lax.axis_size("x") + lax.axis_index("x")
     h = lax.axis_index("c") * half + piece // (chips // half)
     decay = power(wide[h], 2.0 * length)
     running = jnp.zeros(totals.shape[1:], F32)
+
+    def copy(part):
+        pieces = pl.ds(part * (chips // PARTS), chips // PARTS)
+        return pltpu.make_async_copy(prefixes.at[pieces], prefixes_hbm.at[pieces], sems.at[part])
+
     for i in range(chips):
         prefixes[i] = running
         running = running * decay + totals[i]
+        if (i + 1) % (chips // PARTS) == 0:
+            copy(i // (chips // PARTS)).start()
+    for part in range(PARTS):
+        copy(part).wait()
 
 
 def two_halves(matrix):
@@ -228,15 +247,24 @@
         moved=DECAY_MOVED,
         name="positions",
     )()
-    state, given, wide = call(
+    scaled, wide = call(
+        functools.partial(keys_kernel, count, heads),
+        (shape((heads, E, length), BF16), shape((heads, 8, E), F32)),
+        [VMEM] * 3,
+        (VMEM, VMEM),
+        flops=2 * length * E * width,
+        moved=4 * length * width,
+        name="keys",
+    )(inner, decay_rates.reshape(1, heads), key_rows)
+    state, given = call(
         functools.partial(states_kernel, count, heads),
-        (shape((heads, E, E), F32), shape((half, E, E), F32), shape((heads, 8, E), F32)),
-        [VMEM] * 4,
-        (VMEM,) * 3,
+        (shape((heads, E, E), F32), shape((half, E, E), F32)),
+        [VMEM] * 3,
+        (VMEM, VMEM),
         flops=2 * length * E * width,
         moved=4 * length * width,
         name="states",
-    )(inner, decay_rates.reshape(1, heads), key_rows, value_rows)
+    )(wide, scaled, value_rows)
     both = lax.all_gather(given, "c")
     total, first = call(
         functools.partial(chip_kernel, length, half),
@@ -250,7 +278,8 @@
         functools.partial(scan_kernel, length, half, chips),
         shape(owned.shape, F32),
         [VMEM, VMEM],
-        VMEM,
+        HBM,
+        [pltpu.VMEM(owned.shape, F32), pltpu.SemaphoreType.DMA((PARTS,))],
         name="scan",
     )(wide, owned)
     mine = lax.all_to_all(prefixes, CHIPS, 0, 0, tiled=True).reshape(half, E, E)

time: 62.2 us -> 62.1 us (level)
  no operation moved by 1% of the time
where the time goes in v8:
time: 62.1 us; the launch traced here: 61.8 us
  blocking collectives  43.7 us (70%)
  Pallas kernels  6.35 us (10%)
  waiting for transfers between devices  4.43 us (7%)
  starting transfers between devices  3.9 us (6%)
  local copies, waits for them, and re-layouts  3.3 us (5%)
    all_to_all x1, blocking collectives, body(): owned = lax.all_to_all(total.reshape(chips, -1, E), CHIPS, 0, 0, tiled=True)  16.7 us
    all_to_all x1, blocking collectives, body(): shared = lax.all_to_all(squares, HEAD, 0, 0, tiled=True)  13.6 us
    all_gather x1, blocking collectives, body(): both = lax.all_gather(given, 'c')  8.47 us
    all_gather x1, blocking collectives, body(): prefix = lax.all_gather(given, 'c', tiled=True)  5.02 us
    all_to_all x1, waiting for transfers between devices, body(): mine = lax.all_to_all(prefixes, CHIPS, 0, 0, tiled=True).reshape(half, E, E)  4.43 us
    all_to_all x1, starting transfers between devices, body(): mine = lax.all_to_all(prefixes, CHIPS, 0, 0, tiled=True).reshape(half, E, E)  3.9 us
    unnamed x18, local copies, waits for them, and re-layouts  3.3 us
    pallas_call x1, Pallas kernels, body(): call(functools.partial(local_kernel, count, heads), shape((length, width)...  2.57 us
  transfers between devices with their start and end apart: 1, of which 1 were waited for; matrix products, arithmetic and copies ran while one was open for 0% of the time, Pallas kernels for 5%

profile of v8, /device:TPU:1, one launch (start us, length us, event | category | flops | bytes accessed | tf_op | source)
XLA Modules:
  0.0 61.8 jit_solution(4161363340579666103)
XLA Ops:
  0.0 0.0 copy-start
  0.0 0.0 copy-start.8
  0.0 0.0 copy-start.1
  0.0 1.2 %copy-done = bf16[1024,512]{1,0:T(8,128)(2,1)S(1)} copy-done((bf16[1024,512]{1,0:T(8,128)(2,1)S(1)}, bf16[1024,512]{1,0:T(8,128)(2,1)}, u32[]{:S(2)}) %copy-start) | copy-done | bytes 1048600
  1.2 0.0 copy-done.8
  1.2 0.4 keys.3
  1.6 0.0 copy-done.1
  1.6 0.4 states.1
  2.0 8.5 %all-gather = f32[4,128,128]{2,1,0:T(8,128)S(1)} all-gather(f32[2,128,128]{2,1,0:T(8,128)S(1)} %get-tuple-element.24), channel_id=2, replica_groups=mesh['z'=8,'x'=4,'c'=2,'head'=8] {'c'}, dimensions={0}, use_global_device_ids=true | all-gather | bytes 393216 | tf_op jit(solution)/shard_map/all_gather | solution.py:268
  10.6 16.7 %all_to_all.15.totals = f32[32,8,128]{2,1,0:T(8,128)S(1)} all-to-all(f32[32,8,128]{2,1,0:T(8,128)S(1)} %bitcast.8), channel_id=1, replica_groups=mesh['z'=8,'x'=4,'c'=2,'head'=8] {'z','x'}, dimensions={0} | all-to-all | bytes 262144 | tf_op jit(solution)/shard_map/all_to_all | solution.py:276
  27.2 0.7 %scan.1 = f32[32,8,128]{2,1,0:T(8,128)} custom-call(f32[4,8,128]{2,1,0:T(8,128)S(1)} %get-tuple-element.17.wide, f32[32,8,128]{2,1,0:T(8,128)S(1)} %all_to_all.15.totals), custom_call_target="tpu_custom_call" | custom-call | tf_op jit(solution)/shard_map/scan/pallas_call | solution.py:277
  28.0 3.9 %all-to-all-start.1 = ((f32[32,8,128]{2,1,0:T(8,128)}), f32[32,8,128]{2,1,0:T(8,128)S(1)}, u32[]{:S(2)}, u32[]{:S(2)}) async-start(f32[32,8,128]{2,1,0:T(8,128)} %scan.1), calls=%async_computation.1 | async-start | bytes 262144 | tf_op jit(solution)/shard_map/all_to_all | solution.py:285
  31.9 0.0 copy-start.2
  31.9 0.0 copy-start.3
  31.9 0.2 decays.1
  32.1 1.0 %copy-done.2 = bf16[1024,512]{1,0:T(8,128)(2,1)S(1)} copy-done((bf16[1024,512]{1,0:T(8,128)(2,1)S(1)}, bf16[1024,512]{1,0:T(8,128)(2,1)}, u32[]{:S(2)}) %copy-start.2) | copy-done | bytes 1048600
  33.1 0.3 copy-done.3
  33.4 2.6 %local.1 = f32[1024,512]{1,0:T(8,128)S(1)} custom-call(f32[4,8,128]{2,1,0:T(8,128)S(1)} %get-tuple-element.17.wide, f32[4,128,128]{2,1,0:T(8,128)S(1)} %get-tuple-element.19.within, f32[4,128,128]{2,1,0:T(8,128)S(1)} %get-tuple-element.20.across, f32[4,256,128]{2,1,0:T(8,128)S(1)} %get-tuple-element.18.scale, ...), custom_call_target="tpu_custom_call" | custom-call | flops 1073741824 | bytes 5242880 | tf_op jit(solution)/shard_map/local/pallas_call | solution.py:310
  36.0 0.0 copy-start.5
  36.0 0.8 %copy-done.5 = f32[4,256,128]{2,1,0:T(8,128)} copy-done((f32[4,256,128]{2,1,0:T(8,128)}, f32[4,256,128]{2,1,0:T(8,128)S(1)}, u32[]{:S(2)}) %copy-start.5) | copy-done | bytes 524312
  36.8 4.4 %all-to-all-done.1 = f32[32,8,128]{2,1,0:T(8,128)S(1)} async-done(((f32[32,8,128]{2,1,0:T(8,128)}), f32[32,8,128]{2,1,0:T(8,128)S(1)}, u32[]{:S(2)}, u32[]{:S(2)}) %all-to-all-start.1) | async-done | bytes 131104 | tf_op jit(solution)/shard_map/all_to_all | solution.py:285
  41.2 0.0 copy-start.4
  41.2 0.0 copy-start.6
  41.2 0.0 copy-start.7
  41.3 5.0 %all_gather.11.prefix = f32[4,128,128]{2,1,0:T(8,128)S(1)} all-gather(f32[2,128,128]{2,1,0:T(8,128)S(1)} %relay.1), channel_id=1, replica_groups=mesh['z'=8,'x'=4,'c'=2,'head'=8] {'c'}, dimensions={0}, use_global_device_ids=true | all-gather | bytes 393216 | tf_op jit(solution)/shard_map/all_gather | solution.py:295
  46.3 0.0 copy-done.4
  46.3 0.0 copy-done.6
  46.3 0.0 copy-done.7
  46.3 0.8 %mix.1 = (f32[1024,512]{1,0:T(8,128)S(1)}, f32[8,8,128]{2,1,0:T(8,128)S(1)}) custom-call(f32[4,8,128]{2,1,0:T(8,128)S(1)} %get-tuple-element.17.wide, f32[4,256,128]{2,1,0:T(8,128)S(1)} %copy-done.6, bf16[1024,512]{1,0:T(8,128)(2,1)S(1)} %copy-done.4, f32[1024,512]{1,0:T(8,128)S(1)} %local.1, f32[2,128,128]{2,1,0:T(8,128)S(1)} %bitcast.7, ...), custom_call_target="tpu_custom_call" | custom-call | flops 268435456 | bytes 5242880 | tf_op jit(solution)/shard_map/mix/pallas_call | solution.py:321
  47.1 13.6 %all_to_all.16.squares = f32[8,8,128]{2,1,0:T(8,128)S(1)} all-to-all(f32[8,8,128]{2,1,0:T(8,128)S(1)} %get-tuple-element.28), channel_id=1, replica_groups=mesh['z'=8,'x'=4,'c'=2,'head'=8] {'head'}, dimensions={0} | all-to-all | bytes 65536 | tf_op jit(solution)/shard_map/all_to_all | solution.py:330
  60.7 1.1 %norm.1 = bf16[1024,512]{1,0:T(8,128)(2,1)} custom-call(f32[1024,512]{1,0:T(8,128)S(1)} %get-tuple-element.27.mixed, f32[8,8,128]{2,1,0:T(8,128)S(1)} %all_to_all.16.squares), custom_call_target="tpu_custom_call" | custom-call | bytes 3145728 | tf_op jit(solution)/shard_map/norm/pallas_call | solution.py:331
  (3 shorter events, 0.1 us)
Async XLA Ops:
  0.0 1.2 %copy-start = (bf16[1024,512]{1,0:T(8,128)(2,1)S(1)}, bf16[1024,512]{1,0:T(8,128)(2,1)}, u32[]{:S(2)}) copy-start(bf16[1024,512]{1,0:T(8,128)(2,1)} %keys.5) | copy-start | bytes 3145732
  0.0 1.2 %copy-start.8 = (f32[4]{0:T(128)S(1)}, f32[4]{0:T(128)}, u32[]{:S(2)}) copy-start(f32[4]{0:T(128)} %param.8) | copy-start | bytes 52
  0.0 1.6 %copy-start.1 = (bf16[1024,512]{1,0:T(8,128)(2,1)S(1)}, bf16[1024,512]{1,0:T(8,128)(2,1)}, u32[]{:S(2)}) copy-start(bf16[1024,512]{1,0:T(8,128)(2,1)} %values.3) | copy-start | bytes 3145732
  28.0 13.2 %all-to-all-start.1 = ((f32[32,8,128]{2,1,0:T(8,128)}), f32[32,8,128]{2,1,0:T(8,128)S(1)}, u32[]{:S(2)}, u32[]{:S(2)}) async-start(f32[32,8,128]{2,1,0:T(8,128)} %scan.1), calls=%async_computation.1 | async-start | bytes 262144 | tf_op jit(solution)/shard_map/all_to_all | solution.py:285
  31.9 1.2 %copy-start.2 = (bf16[1024,512]{1,0:T(8,128)(2,1)S(1)}, bf16[1024,512]{1,0:T(8,128)(2,1)}, u32[]{:S(2)}) copy-start(bf16[1024,512]{1,0:T(8,128)(2,1)} %values.3) | copy-start | bytes 3145732
  31.9 1.5 %copy-start.3 = (bf16[1024,512]{1,0:T(8,128)(2,1)S(1)}, bf16[1024,512]{1,0:T(8,128)(2,1)}, u32[]{:S(2)}) copy-start(bf16[1024,512]{1,0:T(8,128)(2,1)} %queries.3) | copy-start | bytes 3145732
  36.0 0.8 %copy-start.5 = (f32[4,256,128]{2,1,0:T(8,128)}, f32[4,256,128]{2,1,0:T(8,128)S(1)}, u32[]{:S(2)}) copy-start(f32[4,256,128]{2,1,0:T(8,128)S(1)} %get-tuple-element.18.scale) | copy-start | bytes 1572868
  41.2 5.1 %copy-start.4 = (bf16[1024,512]{1,0:T(8,128)(2,1)S(1)}, bf16[1024,512]{1,0:T(8,128)(2,1)}, u32[]{:S(2)}) copy-start(bf16[1024,512]{1,0:T(8,128)(2,1)} %queries.3) | copy-start | bytes 3145732
  41.2 5.1 %copy-start.6 = (f32[4,256,128]{2,1,0:T(8,128)S(1)}, f32[4,256,128]{2,1,0:T(8,128)}, u32[]{:S(2)}) copy-start(f32[4,256,128]{2,1,0:T(8,128)} %copy-done.5) | copy-start | bytes 1572868
  41.2 5.1 %copy-start.7 = (f32[512]{0:T(512)S(1)}, f32[512]{0:T(512)}, u32[]{:S(2)}) copy-start(f32[512]{0:T(512)} %param.9) | copy-start | bytes 6148

commit v9 on v6

--- a/solution.py
+++ b/solution.py
@@ -192,10 +192,12 @@
         for h in range(out.shape[1] // E):
             part = mixed[rows, head_columns(h)] * column
             out[rows, head_columns(h)] = part.astype(BF16)
-        pltpu.make_async_copy(out.at[rows], out_hbm.at[rows], sems.at[t]).start()
-    for t in range(tiles):
-        rows = pl.ds(t * E, E)
-        pltpu.make_async_copy(out.at[rows], out_hbm.at[rows], sems.at[t]).wait()
+        if t % 2 == 1:
+            pair = pl.ds((t - 1) * E, 2 * E)
+            pltpu.make_async_copy(out.at[pair], out_hbm.at[pair], sems.at[t // 2]).start()
+    for t in range(1, tiles, 2):
+        pair = pl.ds((t - 1) * E, 2 * E)
+        pltpu.make_async_copy(out.at[pair], out_hbm.at[pair], sems.at[t // 2]).wait()
 
 
 def body(queries, key_rows, value_rows, decay_rates, out_gain):
@@ -292,7 +294,7 @@
         shape((length, width), BF16),
         [VMEM, VMEM],
         HBM,
-        [pltpu.VMEM((length, width), BF16), pltpu.SemaphoreType.DMA((length // E,))],
+        [pltpu.VMEM((length, width), BF16), pltpu.SemaphoreType.DMA((count,))],
         moved=6 * length * width,
         name="norm",
     )(mixed, shared)

time: 62.3 us -> 62.3 us (level)
  no operation moved by 1% of the time
where the time goes in v9:
time: 62.3 us; the launch traced here: 62 us
  blocking collectives  44 us (71%)
  Pallas kernels  5.93 us (10%)
  waiting for transfers between devices  5.02 us (8%)
  starting transfers between devices  3.88 us (6%)
  local copies, waits for them, and re-layouts  3.13 us (5%)
    all_to_all x1, blocking collectives, body(): owned = lax.all_to_all(total.reshape(chips, -1, E), CHIPS, 0, 0, tiled=True)  16.7 us
    all_to_all x1, blocking collectives, body(): shared = lax.all_to_all(squares, HEAD, 0, 0, tiled=True)  13.6 us
    all_gather x1, blocking collectives, body(): both = lax.all_gather(state, 'c')  8.65 us
    all_gather x1, blocking collectives, body(): prefix = lax.all_gather(mine, 'c', tiled=True)  5.09 us
    all_to_all x1, waiting for transfers between devices, body(): mine = lax.all_to_all(prefixes, CHIPS, 0, 0, tiled=True).reshape(half, E, E)  5.02 us
    all_to_all x1, starting transfers between devices, body(): mine = lax.all_to_all(prefixes, CHIPS, 0, 0, tiled=True).reshape(half, E, E)  3.88 us
    unnamed x16, local copies, waits for them, and re-layouts  3.13 us
    pallas_call x1, Pallas kernels, body(): call(functools.partial(local_kernel, count, heads), shape((length, width)...  2.46 us
  transfers between devices with their start and end apart: 1, of which 1 were waited for; matrix products, arithmetic and copies ran while one was open for 0% of the time, Pallas kernels for 4%

profile of v9, /device:TPU:1, one launch (start us, length us, event | category | flops | bytes accessed | tf_op | source)
XLA Modules:
  0.0 62.0 jit_solution(11274210482156762013)
XLA Ops:
  0.0 0.0 copy-start.4
  0.0 0.0 copy-start.2
  0.0 0.0 copy-start.7
  0.0 1.2 %copy-done.4 = bf16[1024,512]{1,0:T(8,128)(2,1)S(1)} copy-done((bf16[1024,512]{1,0:T(8,128)(2,1)S(1)}, bf16[1024,512]{1,0:T(8,128)(2,1)}, u32[]{:S(2)}) %copy-start.4) | copy-done | bytes 1048600
  1.2 0.3 copy-done.2
  1.5 0.0 copy-done.7
  1.5 0.5 states.1
  2.1 8.6 %all-gather = f32[8,128,128]{2,1,0:T(8,128)S(1)} all-gather(f32[4,128,128]{2,1,0:T(8,128)S(1)} %get-tuple-element.18), channel_id=2, replica_groups=mesh['z'=8,'x'=4,'c'=2,'head'=8] {'c'}, dimensions={0}, use_global_device_ids=true | all-gather | bytes 786432 | tf_op jit(solution)/shard_map/all_gather | solution.py:230
  10.8 16.7 %all_to_all.15.totals = f32[32,8,128]{2,1,0:T(8,128)S(1)} all-to-all(f32[32,8,128]{2,1,0:T(8,128)S(1)} %bitcast.7), channel_id=1, replica_groups=mesh['z'=8,'x'=4,'c'=2,'head'=8] {'z','x'}, dimensions={0} | all-to-all | bytes 262144 | tf_op jit(solution)/shard_map/all_to_all | solution.py:238
  27.4 0.7 %scan.1 = f32[32,8,128]{2,1,0:T(8,128)} custom-call(f32[4,8,128]{2,1,0:T(8,128)S(1)} %get-tuple-element.13.wide, f32[32,8,128]{2,1,0:T(8,128)S(1)} %all_to_all.15.totals), custom_call_target="tpu_custom_call" | custom-call | tf_op jit(solution)/shard_map/scan/pallas_call | solution.py:239
  28.2 3.9 %all-to-all-start.1 = ((f32[32,8,128]{2,1,0:T(8,128)}), f32[32,8,128]{2,1,0:T(8,128)S(1)}, u32[]{:S(2)}, u32[]{:S(2)}) async-start(f32[32,8,128]{2,1,0:T(8,128)} %scan.1), calls=%async_computation.1 | async-start | bytes 262144 | tf_op jit(solution)/shard_map/all_to_all | solution.py:246
  32.1 0.0 copy-start
  32.1 0.0 copy-start.3
  32.1 0.0 copy-start.5
  32.1 0.2 decays.1
  32.4 0.9 %copy-done = bf16[1024,512]{1,0:T(8,128)(2,1)S(1)} copy-done((bf16[1024,512]{1,0:T(8,128)(2,1)S(1)}, bf16[1024,512]{1,0:T(8,128)(2,1)}, u32[]{:S(2)}) %copy-start) | copy-done | bytes 1048600
  33.3 0.3 copy-done.3
  33.6 0.3 copy-done.5
  33.9 2.5 %local.1 = f32[1024,512]{1,0:T(8,128)S(1)} custom-call(f32[4,8,128]{2,1,0:T(8,128)S(1)} %get-tuple-element.13.wide, f32[4,128,128]{2,1,0:T(8,128)S(1)} %get-tuple-element.15.within, f32[4,128,128]{2,1,0:T(8,128)S(1)} %get-tuple-element.16.across, f32[4,256,128]{2,1,0:T(8,128)S(1)} %get-tuple-element.14.scale, ...), custom_call_target="tpu_custom_call" | custom-call | flops 1073741824 | bytes 5242880 | tf_op jit(solution)/shard_map/local/pallas_call | solution.py:271
  36.4 5.0 %all-to-all-done.1 = f32[32,8,128]{2,1,0:T(8,128)S(1)} async-done(((f32[32,8,128]{2,1,0:T(8,128)}), f32[32,8,128]{2,1,0:T(8,128)S(1)}, u32[]{:S(2)}, u32[]{:S(2)}) %all-to-all-start.1) | async-done | bytes 131104 | tf_op jit(solution)/shard_map/all_to_all | solution.py:246
  41.4 0.0 copy-start.1
  41.4 0.0 copy-start.6
  41.4 5.1 %all_gather.11.prefix = f32[4,128,128]{2,1,0:T(8,128)S(1)} all-gather(f32[2,128,128]{2,1,0:T(8,128)S(1)} %relay.1), channel_id=1, replica_groups=mesh['z'=8,'x'=4,'c'=2,'head'=8] {'c'}, dimensions={0}, use_global_device_ids=true | all-gather | bytes 393216 | tf_op jit(solution)/shard_map/all_gather | solution.py:256
  46.5 0.0 copy-done.1
  46.5 0.0 copy-done.6
  46.5 0.8 %mix.1 = (f32[1024,512]{1,0:T(8,128)S(1)}, f32[8,8,128]{2,1,0:T(8,128)S(1)}) custom-call(f32[4,8,128]{2,1,0:T(8,128)S(1)} %get-tuple-element.13.wide, f32[4,256,128]{2,1,0:T(8,128)S(1)} %get-tuple-element.14.scale, bf16[1024,512]{1,0:T(8,128)(2,1)S(1)} %copy-done.1, f32[1024,512]{1,0:T(8,128)S(1)} %local.1, f32[4,128,128]{2,1,0:T(8,128)S(1)} %all_gather.11.prefix, ...), custom_call_target="tpu_custom_call" | custom-call | flops 268435456 | bytes 5242880 | tf_op jit(solution)/shard_map/mix/pallas_call | solution.py:282
  47.3 13.6 %all_to_all.16.squares = f32[8,8,128]{2,1,0:T(8,128)S(1)} all-to-all(f32[8,8,128]{2,1,0:T(8,128)S(1)} %get-tuple-element.20), channel_id=1, replica_groups=mesh['z'=8,'x'=4,'c'=2,'head'=8] {'head'}, dimensions={0} | all-to-all | bytes 65536 | tf_op jit(solution)/shard_map/all_to_all | solution.py:291
  60.9 1.1 %norm.1 = bf16[1024,512]{1,0:T(8,128)(2,1)} custom-call(f32[1024,512]{1,0:T(8,128)S(1)} %get-tuple-element.19.mixed, f32[8,8,128]{2,1,0:T(8,128)S(1)} %all_to_all.16.squares), custom_call_target="tpu_custom_call" | custom-call | bytes 3145728 | tf_op jit(solution)/shard_map/norm/pallas_call | solution.py:292
  (3 shorter events, 0.0 us)
Async XLA Ops:
  0.0 1.2 %copy-start.4 = (bf16[1024,512]{1,0:T(8,128)(2,1)S(1)}, bf16[1024,512]{1,0:T(8,128)(2,1)}, u32[]{:S(2)}) copy-start(bf16[1024,512]{1,0:T(8,128)(2,1)} %values.3) | copy-start | bytes 3145732
  0.0 1.5 %copy-start.2 = (bf16[1024,512]{1,0:T(8,128)(2,1)S(1)}, bf16[1024,512]{1,0:T(8,128)(2,1)}, u32[]{:S(2)}) copy-start(bf16[1024,512]{1,0:T(8,128)(2,1)} %keys.3) | copy-start | bytes 3145732
  0.0 1.5 %copy-start.7 = (f32[4]{0:T(128)S(1)}, f32[4]{0:T(128)}, u32[]{:S(2)}) copy-start(f32[4]{0:T(128)} %param.8) | copy-start | bytes 52
  28.2 13.2 %all-to-all-start.1 = ((f32[32,8,128]{2,1,0:T(8,128)}), f32[32,8,128]{2,1,0:T(8,128)S(1)}, u32[]{:S(2)}, u32[]{:S(2)}) async-start(f32[32,8,128]{2,1,0:T(8,128)} %scan.1), calls=%async_computation.1 | async-start | bytes 262144 | tf_op jit(solution)/shard_map/all_to_all | solution.py:246
  32.1 1.2 %copy-start = (bf16[1024,512]{1,0:T(8,128)(2,1)S(1)}, bf16[1024,512]{1,0:T(8,128)(2,1)}, u32[]{:S(2)}) copy-start(bf16[1024,512]{1,0:T(8,128)(2,1)} %queries.3) | copy-start | bytes 3145732
  32.1 1.5 %copy-start.3 = (bf16[1024,512]{1,0:T(8,128)(2,1)S(1)}, bf16[1024,512]{1,0:T(8,128)(2,1)}, u32[]{:S(2)}) copy-start(bf16[1024,512]{1,0:T(8,128)(2,1)} %keys.3) | copy-start | bytes 3145732
  32.1 1.8 %copy-start.5 = (bf16[1024,512]{1,0:T(8,128)(2,1)S(1)}, bf16[1024,512]{1,0:T(8,128)(2,1)}, u32[]{:S(2)}) copy-start(bf16[1024,512]{1,0:T(8,128)(2,1)} %values.3) | copy-start | bytes 3145732
  41.4 5.1 %copy-start.1 = (bf16[1024,512]{1,0:T(8,128)(2,1)S(1)}, bf16[1024,512]{1,0:T(8,128)(2,1)}, u32[]{:S(2)}) copy-start(bf16[1024,512]{1,0:T(8,128)(2,1)} %queries.3) | copy-start | bytes 3145732
  41.4 5.1 %copy-start.6 = (f32[512]{0:T(512)S(1)}, f32[512]{0:T(512)}, u32[]{:S(2)}) copy-start(f32[512]{0:T(512)} %param.9) | copy-start | bytes 6148
